TPU v7x, 256 devices: a whole 4x4x8 slice. The times are simulated.
256 devices in a mesh: blk: 8 (over x_lo, y), freq: 32 (over x_hi, z, core).
Axes of the slice: x: 4 (x_hi: 2, x_lo: 2; x = x_hi * 2 + x_lo), y: 4, z: 8, core: 2. Of those that a mesh axis runs over, the one named last changes fastest.
Arguments:
- spectra: bfloat16 [2048, 2, 4096], P('blk', None, 'freq'), may hold values from -180 to 180
- pair_first: int32 [8, 8, 2048], P('blk'), may hold values from 0 to 255
- pair_second: int32 [8, 8, 2048], P('blk'), may hold values from 0 to 255
- pair_bin: int32 [8, 8, 2048], P('blk'), may hold values from 0 to 63, as said below
- bin_owner: int32 [64], replicated, may hold values from 0 to 7, as said below
Outputs:
- correlation: float32 [4096, 128], P('freq', 'blk')
Inputs may be any that keep to these rules, and one draw needn't show every extreme that they name: Each list pair_bin[a, r] is nondecreasing along its last dimension, starts with 0 and ends with 63. `bin_owner`: each block index owns at most 16 bins, and some index owns exactly 16.
All inputs are finite; a program needn't handle non-finite values.
Results may differ from a plain program's by a relative error of at most 0.0049.
Values may be sent and summed in bfloat16 or wider, within the bound.
No kernel may reach another device: no remote copies, remote signals or barrier semaphores. Data moves between devices by JAX's collectives and lax.ppermute only.
A program may use at most 64 MiB of HBM per device.

v0:
```python
import math

import jax
import jax.numpy as jnp
from jax import lax
from jax.sharding import PartitionSpec as P

F = 4096
NB = 64
PAIRS = 2048


def from_behind(x, axis, by):
    devices = lax.axis_size(axis)
    return lax.ppermute(x, axis, [(i, (i + by) % devices) for i in range(devices)])


def cross_stack(total, white, remote, first_rows, second_rows, bin_rows):
    left = white[first_rows].astype(jnp.float32)
    right = remote[second_rows].astype(jnp.float32)
    real_part = left[:, 0] * right[:, 0] + left[:, 1] * right[:, 1]
    imag_part = left[:, 1] * right[:, 0] - left[:, 0] * right[:, 1]
    cross = jnp.stack([real_part, imag_part], 1).astype(jnp.bfloat16)
    onehot = (bin_rows[None, :] == jnp.arange(NB, dtype=jnp.int32)[:, None]).astype(jnp.bfloat16)
    flat = cross.reshape(cross.shape[0], -1)
    return total + jnp.dot(onehot, flat, preferred_element_type=jnp.float32)


def lag_block(lag_rows, freq_rows, piece):
    phase = (lag_rows[:, None] * freq_rows[None, :] % F).astype(jnp.float32) * (2.0 * math.pi / F)
    line = jnp.dot(jnp.cos(phase), piece[:, 0, :].T, precision=lax.Precision.HIGHEST)
    return line - jnp.dot(jnp.sin(phase), piece[:, 1, :].T, precision=lax.Precision.HIGHEST)


def on_device(spectra, pair_first, pair_second, pair_bin, bin_owner):
    blocks = lax.axis_size("blk")
    freq_dev = spectra.shape[2]
    values = spectra.astype(jnp.float32)
    power = lax.psum(jnp.sum(values * values, axis=(1, 2)), "freq")
    rms = jnp.sqrt(power / (2 * F) + 1e-06)
    white = (values / rms[:, None, None]).astype(jnp.bfloat16)
    total = jnp.zeros((NB, 2 * freq_dev), jnp.float32)
    remote = white
    for step_count in range(blocks):
        if step_count > 0:
            remote = from_behind(remote, "blk", 1)
        total = cross_stack(
            total,
            white,
            remote,
            pair_first[0, step_count],
            pair_second[0, step_count],
            pair_bin[0, step_count],
        )
    partial_stack = total.reshape(NB, 2, freq_dev)
    slots_each = 2 * NB // blocks
    bins = jnp.arange(NB, dtype=jnp.int32)
    same = bin_owner[:, None] == bin_owner[None, :]
    lower = bins[None, :] < bins[:, None]
    rank = jnp.sum((same & lower).astype(jnp.int32), axis=1)
    slot = bin_owner * slots_each + rank
    totals = lax.psum(partial_stack, "blk")
    mine = lax.axis_index("blk")
    wanted = mine * slots_each + jnp.arange(slots_each, dtype=jnp.int32)
    select = (slot[None, :] == wanted[:, None]).astype(jnp.float32)
    owned = jnp.einsum("sb,bcf->scf", select, totals, precision=lax.Precision.HIGHEST)
    freq_index = lax.axis_index("freq")
    scale = (F * PAIRS * blocks * blocks / NB) ** (-0.5)
    lag_rows = jnp.arange(freq_dev * lax.axis_size("freq"), dtype=jnp.int32)
    freq_rows = freq_index * freq_dev + jnp.arange(freq_dev, dtype=jnp.int32)
    line = lax.psum_scatter(
        lag_block(lag_rows, freq_rows, owned), "freq", scatter_dimension=0, tiled=True
    )
    return line * scale


def solution(mesh):
    return jax.shard_map(
        on_device,
        mesh=mesh,
        in_specs=(
            P("blk", None, "freq"),
            P("blk", None, None),
            P("blk", None, None),
            P("blk", None, None),
            P(),
        ),
        out_specs=P("freq", "blk"),
        check_vma=False,
    )
```

profile of v0, /device:TPU:8, one launch (start us, length us, event | category | flops | bytes accessed | tf_op | source)
XLA Modules:
  0.0 524.1 jit_solution(14951603235629611911)
XLA Ops:
  8.5 72.8 %psum.14 = f32[256]{0:T(256)S(1)} all-reduce(f32[256]{0:T(256)S(1)} %fusion.29), channel_id=1, replica_groups=mesh['blk'=8,'freq'=32] {'freq'}, use_global_device_ids=true, to_apply=%region_2.0 | all-reduce | flops 256 | bytes 2048 | tf_op jit(solution)/shard_map/psum | solution.py:39
  85.5 7.1 %gather_fusion = bf16[2048,2,128]{2,1,0:T(2,128)(2,1)S(1)} fusion(bf16[256,2,128]{2,1,0:T(2,128)(2,1)S(1)} %fusion.30, s32[2048]{0:T(1024)S(1)} %broadcast_clamp_fusion.15), kind=kCustom, calls=%fused_computation | custom fusion | bytes 2105344 | tf_op jit(solution)/shard_map/gather | solution.py:19
  93.5 7.0 %gather_fusion.1 = bf16[2048,2,128]{2,1,0:T(2,128)(2,1)S(1)} fusion(bf16[256,2,128]{2,1,0:T(2,128)(2,1)S(1)} %fusion.30, s32[2048]{0:T(1024)S(1)} %broadcast_clamp_fusion.14), kind=kCustom, calls=%fused_computation.1 | custom fusion | bytes 2105344 | tf_op jit(solution)/shard_map/gather | solution.py:20
  109.1 7.0 %gather_fusion.2 = bf16[2048,2,128]{2,1,0:T(2,128)(2,1)S(1)} fusion(bf16[256,2,128]{2,1,0:T(2,128)(2,1)S(1)} %fusion.30, s32[2048]{0:T(1024)S(1)} %broadcast_clamp_fusion.13), kind=kCustom, calls=%fused_computation.2 | custom fusion | bytes 2105344 | tf_op jit(solution)/shard_map/gather | solution.py:19
  117.9 7.0 %gather_fusion.4 = bf16[2048,2,128]{2,1,0:T(2,128)(2,1)S(1)} fusion(bf16[256,2,128]{2,1,0:T(2,128)(2,1)S(1)} %fusion.30, s32[2048]{0:T(1024)S(1)} %broadcast_clamp_fusion.11), kind=kCustom, calls=%fused_computation.4 | custom fusion | bytes 2105344 | tf_op jit(solution)/shard_map/gather | solution.py:19
  126.7 7.0 %gather_fusion.6 = bf16[2048,2,128]{2,1,0:T(2,128)(2,1)S(1)} fusion(bf16[256,2,128]{2,1,0:T(2,128)(2,1)S(1)} %fusion.30, s32[2048]{0:T(1024)S(1)} %broadcast_clamp_fusion.9), kind=kCustom, calls=%fused_computation.6 | custom fusion | bytes 2105344 | tf_op jit(solution)/shard_map/gather | solution.py:19
  135.6 7.0 %gather_fusion.8 = bf16[2048,2,128]{2,1,0:T(2,128)(2,1)S(1)} fusion(bf16[256,2,128]{2,1,0:T(2,128)(2,1)S(1)} %fusion.30, s32[2048]{0:T(1024)S(1)} %broadcast_clamp_fusion.7), kind=kCustom, calls=%fused_computation.8 | custom fusion | bytes 2105344 | tf_op jit(solution)/shard_map/gather | solution.py:19
  144.4 7.0 %gather_fusion.10 = bf16[2048,2,128]{2,1,0:T(2,128)(2,1)S(1)} fusion(bf16[256,2,128]{2,1,0:T(2,128)(2,1)S(1)} %fusion.30, s32[2048]{0:T(1024)S(1)} %broadcast_clamp_fusion.5), kind=kCustom, calls=%fused_computation.10 | custom fusion | bytes 2105344 | tf_op jit(solution)/shard_map/gather | solution.py:19
  153.2 7.1 %gather_fusion.12 = bf16[2048,2,128]{2,1,0:T(2,128)(2,1)S(1)} fusion(bf16[256,2,128]{2,1,0:T(2,128)(2,1)S(1)} %fusion.30, s32[2048]{0:T(1024)S(1)} %broadcast_clamp_fusion.3), kind=kCustom, calls=%fused_computation.12 | custom fusion | bytes 2105344 | tf_op jit(solution)/shard_map/gather | solution.py:19
  162.0 7.0 %gather_fusion.14 = bf16[2048,2,128]{2,1,0:T(2,128)(2,1)S(1)} fusion(bf16[256,2,128]{2,1,0:T(2,128)(2,1)S(1)} %fusion.30, s32[2048]{0:T(1024)S(1)} %broadcast_clamp_fusion.1), kind=kCustom, calls=%fused_computation.14 | custom fusion | bytes 2105344 | tf_op jit(solution)/shard_map/gather | solution.py:19
  169.9 7.1 %gather_fusion.3 = bf16[2048,2,128]{2,1,0:T(2,128)(2,1)S(1)} fusion(bf16[256,2,128]{2,1,0:T(2,128)(2,1)S(1)} %collective-permute-done, s32[2048]{0:T(1024)S(1)} %broadcast_clamp_fusion.12), kind=kCustom, calls=%fused_computation.3 | custom fusion | bytes 2105344 | tf_op jit(solution)/shard_map/gather | solution.py:20
  189.5 7.0 %gather_fusion.5 = bf16[2048,2,128]{2,1,0:T(2,128)(2,1)S(1)} fusion(bf16[256,2,128]{2,1,0:T(2,128)(2,1)S(1)} %collective-permute-done.1, s32[2048]{0:T(1024)S(1)} %broadcast_clamp_fusion.10), kind=kCustom, calls=%fused_computation.5 | custom fusion | bytes 2105344 | tf_op jit(solution)/shard_map/gather | solution.py:20
  209.5 7.0 %gather_fusion.7 = bf16[2048,2,128]{2,1,0:T(2,128)(2,1)S(1)} fusion(bf16[256,2,128]{2,1,0:T(2,128)(2,1)S(1)} %collective-permute-done.2, s32[2048]{0:T(1024)S(1)} %broadcast_clamp_fusion.8), kind=kCustom, calls=%fused_computation.7 | custom fusion | bytes 2105344 | tf_op jit(solution)/shard_map/gather | solution.py:20
  231.0 7.4 %gather_fusion.9 = bf16[2048,2,128]{2,1,0:T(2,128)(2,1)S(1)} fusion(bf16[256,2,128]{2,1,0:T(2,128)(2,1)S(1)} %collective-permute-done.3, s32[2048]{0:T(1024)S(1)} %broadcast_clamp_fusion.6), kind=kCustom, calls=%fused_computation.9 | custom fusion | bytes 2105344 | tf_op jit(solution)/shard_map/gather | solution.py:20
  246.8 6.1 %collective-permute-done.4 = bf16[256,2,128]{2,1,0:T(2,128)(2,1)S(1)} collective-permute-done((bf16[256,2,128]{2,1,0:T(2,128)(2,1)S(1)}, bf16[256,2,128]{2,1,0:T(2,128)(2,1)S(1)}, u32[]{:S(2)}, u32[]{:S(2)}) %collective-permute-start.4) | collective-permute-done | bytes 131104 | tf_op jit(solution)/shard_map/ppermute | solution.py:15
  253.0 7.0 %gather_fusion.11 = bf16[2048,2,128]{2,1,0:T(2,128)(2,1)S(1)} fusion(bf16[256,2,128]{2,1,0:T(2,128)(2,1)S(1)} %collective-permute-done.4, s32[2048]{0:T(1024)S(1)} %broadcast_clamp_fusion.4), kind=kCustom, calls=%fused_computation.11 | custom fusion | bytes 2105344 | tf_op jit(solution)/shard_map/gather | solution.py:20
  268.4 6.1 %collective-permute-done.5 = bf16[256,2,128]{2,1,0:T(2,128)(2,1)S(1)} collective-permute-done((bf16[256,2,128]{2,1,0:T(2,128)(2,1)S(1)}, bf16[256,2,128]{2,1,0:T(2,128)(2,1)S(1)}, u32[]{:S(2)}, u32[]{:S(2)}) %collective-permute-start.5) | collective-permute-done | bytes 131104 | tf_op jit(solution)/shard_map/ppermute | solution.py:15
  274.5 7.0 %gather_fusion.13 = bf16[2048,2,128]{2,1,0:T(2,128)(2,1)S(1)} fusion(bf16[256,2,128]{2,1,0:T(2,128)(2,1)S(1)} %collective-permute-done.5, s32[2048]{0:T(1024)S(1)} %broadcast_clamp_fusion.2), kind=kCustom, calls=%fused_computation.13 | custom fusion | bytes 2105344 | tf_op jit(solution)/shard_map/gather | solution.py:20
  290.1 6.1 %collective-permute-done.6 = bf16[256,2,128]{2,1,0:T(2,128)(2,1)S(1)} collective-permute-done((bf16[256,2,128]{2,1,0:T(2,128)(2,1)S(1)}, bf16[256,2,128]{2,1,0:T(2,128)(2,1)S(1)}, u32[]{:S(2)}, u32[]{:S(2)}) %collective-permute-start.6) | collective-permute-done | bytes 131104 | tf_op jit(solution)/shard_map/ppermute | solution.py:15
  296.2 7.0 %gather_fusion.15 = bf16[2048,2,128]{2,1,0:T(2,128)(2,1)S(1)} fusion(bf16[256,2,128]{2,1,0:T(2,128)(2,1)S(1)} %collective-permute-done.6, s32[2048]{0:T(1024)S(1)} %broadcast_clamp_fusion), kind=kCustom, calls=%fused_computation.15 | custom fusion | bytes 2105344 | tf_op jit(solution)/shard_map/gather | solution.py:20
  310.9 72.4 %all-reduce.2.cloned.1.call-done = f32[64,2,128]{2,0,1:T(8,128)} async-done(((f32[64,2,128]{2,0,1:T(8,128)}), f32[64,2,128]{2,0,1:T(8,128)}) %all-reduce.2.cloned.1.call-update) | async-done | bytes 65552 | tf_op jit(solution)/shard_map/psum | solution.py:62
  384.3 9.5 %fusion.4 = f32[4096,16]{0,1:T(8,128)S(1)} fusion(s32[128]{0:T(128)S(1)} %iota_add_fusion.1, f32[16,2,128]{2,0,1:T(8,128)S(1)} %fusion.40), kind=kOutput, calls=%fused_computation.24 | convolution fusion | flops 108003328 | bytes 270848 | tf_op jit(solution)/shard_map/dot_general | solution.py:31
  393.8 11.2 %convolution_subtract_fusion = f32[4096,16]{0,1:T(8,128)} fusion(f32[4096,16]{0,1:T(8,128)S(1)} %fusion.4, s32[128]{0:T(128)S(1)} %iota_add_fusion.1, f32[16,2,128]{2,0,1:T(8,128)S(1)} %fusion.40), kind=kOutput, calls=%fused_computation.16 | convolution fusion | flops 108068864 | bytes 532992 | tf_op jit(solution)/shard_map/dot_general | solution.py:32
  405.1 110.6 %reduce-scatter.2.cloned.1.call-done = f32[128,16]{0,1:T(8,128)} async-done(((f32[4096,16]{0,1:T(8,128)}), f32[128,16]{0,1:T(8,128)}) %reduce-scatter.2.cloned.1.call-update) | async-done | bytes 8208 | tf_op jit(solution)/shard_map/reduce_scatter | solution.py:71
  (126 shorter events, 101.6 us)
Async XLA Ops:
  6.5 376.8 %all-reduce.2.cloned.1.call-start = ((), (), s32[]{:S(2)}) async-start(), calls=%async_computation.1 | async-start | bytes 131072 | tf_op jit(solution)/shard_map/psum | solution.py:62
  82.5 87.4 %collective-permute-start = (bf16[256,2,128]{2,1,0:T(2,128)(2,1)S(1)}, bf16[256,2,128]{2,1,0:T(2,128)(2,1)S(1)}, u32[]{:S(2)}, u32[]{:S(2)}) collective-permute-start(bf16[256,2,128]{2,1,0:T(2,128)(2,1)S(1)} %fusion.30), channel_id=1, source_target_pairs={{0,32},{32,64},{64,96},{96,128},{128,160},{160,192},{192,224},{224... | collective-permute-start | bytes 393224 | tf_op jit(solution)/shard_map/ppermute | solution.py:15
  100.6 1.6 copy-start.13
  181.8 4.1 copy-start.12
  181.8 4.1 copy-start.14
  184.5 5.0 collective-permute-start.1
  196.6 1.6 copy-start.4
  201.4 3.9 copy-start.11
  201.5 3.9 copy-start.15
  203.9 5.6 %collective-permute-start.2 = (bf16[256,2,128]{2,1,0:T(2,128)(2,1)S(1)}, bf16[256,2,128]{2,1,0:T(2,128)(2,1)S(1)}, u32[]{:S(2)}, u32[]{:S(2)}) collective-permute-start(bf16[256,2,128]{2,1,0:T(2,128)(2,1)S(1)} %collective-permute-done.1), channel_id=1, source_target_pairs={{0,32},{32,64},{64,96},{96,128},{128,160},{160,192},{192,224},{224... | collective-permute-start | bytes 393224 | tf_op jit(solution)/shard_map/ppermute | solution.py:15
  221.4 3.4 copy-start.10
  221.4 3.4 copy-start.16
  223.9 7.2 %collective-permute-start.3 = (bf16[256,2,128]{2,1,0:T(2,128)(2,1)S(1)}, bf16[256,2,128]{2,1,0:T(2,128)(2,1)S(1)}, u32[]{:S(2)}, u32[]{:S(2)}) collective-permute-start(bf16[256,2,128]{2,1,0:T(2,128)(2,1)S(1)} %collective-permute-done.2), channel_id=1, source_target_pairs={{0,32},{32,64},{64,96},{96,128},{128,160},{160,192},{192,224},{224... | collective-permute-start | bytes 393224 | tf_op jit(solution)/shard_map/ppermute | solution.py:15
  238.5 1.6 copy-start.2
  243.4 2.6 copy-start.9
  243.4 2.6 copy-start.17
  245.8 7.1 %collective-permute-start.4 = (bf16[256,2,128]{2,1,0:T(2,128)(2,1)S(1)}, bf16[256,2,128]{2,1,0:T(2,128)(2,1)S(1)}, u32[]{:S(2)}, u32[]{:S(2)}) collective-permute-start(bf16[256,2,128]{2,1,0:T(2,128)(2,1)S(1)} %collective-permute-done.3), channel_id=1, source_target_pairs={{0,32},{32,64},{64,96},{96,128},{128,160},{160,192},{192,224},{224... | collective-permute-start | bytes 393224 | tf_op jit(solution)/shard_map/ppermute | solution.py:15
  264.9 2.6 copy-start.8
  264.9 2.6 copy-start.18
  267.4 7.2 %collective-permute-start.5 = (bf16[256,2,128]{2,1,0:T(2,128)(2,1)S(1)}, bf16[256,2,128]{2,1,0:T(2,128)(2,1)S(1)}, u32[]{:S(2)}, u32[]{:S(2)}) collective-permute-start(bf16[256,2,128]{2,1,0:T(2,128)(2,1)S(1)} %collective-permute-done.4), channel_id=1, source_target_pairs={{0,32},{32,64},{64,96},{96,128},{128,160},{160,192},{192,224},{224... | collective-permute-start | bytes 393224 | tf_op jit(solution)/shard_map/ppermute | solution.py:15
  286.5 2.7 copy-start.19
  288.9 7.3 %collective-permute-start.6 = (bf16[256,2,128]{2,1,0:T(2,128)(2,1)S(1)}, bf16[256,2,128]{2,1,0:T(2,128)(2,1)S(1)}, u32[]{:S(2)}, u32[]{:S(2)}) collective-permute-start(bf16[256,2,128]{2,1,0:T(2,128)(2,1)S(1)} %collective-permute-done.5), channel_id=1, source_target_pairs={{0,32},{32,64},{64,96},{96,128},{128,160},{160,192},{192,224},{224... | collective-permute-start | bytes 393224 | tf_op jit(solution)/shard_map/ppermute | solution.py:15
  307.4 2.5 copy-start.20
  310.8 204.9 %reduce-scatter.2.cloned.1.call-start = ((), (), s32[]{:S(2)}) async-start(), calls=%async_computation.2 | async-start | bytes 270336 | tf_op jit(solution)/shard_map/reduce_scatter | solution.py:71
  (6 other events, 8.1 us)
Sparse Core Ops, SparseCore 0:
  310.9 72.3 all-reduce.1
  405.2 110.4 reduce-scatter.1
where the time goes:
time: 534 us; the launch traced here: 524 us
  waiting for transfers between devices  213 us (40%)
  local copies, waits for them, and re-layouts  119 us (22%)
  blocking collectives  72.8 us (14%)
  other arithmetic  70.4 us (13%)
  matrix products  28.5 us (5%)
  between operations  14.4 us (3%)
  starting transfers between devices  5.91 us (1%)
    reduce_scatter x1, waiting for transfers between devices, on_device(): lax.psum_scatter(lag_block(lag_rows, freq_rows, owned), 'freq', scatter_d...  111 us
    psum x1, blocking collectives, on_device(): power = lax.psum(jnp.sum(values * values, axis=(1, 2)), 'freq')  72.8 us
    psum x1, waiting for transfers between devices, on_device(): totals = lax.psum(partial_stack, 'blk')  72.4 us
    gather x8, local copies, waits for them, and re-layouts, cross_stack(): right = remote[second_rows].astype(jnp.float32)  56.8 us
    gather x8, local copies, waits for them, and re-layouts, cross_stack(): left = white[first_rows].astype(jnp.float32)  56.4 us
    ppermute x7, waiting for transfers between devices, from_behind(): lax.ppermute(x, axis, [(i, (i + by) % devices) for i in range(devices)])  29.6 us
    another operation x8, other arithmetic  26.3 us
    another operation x8, other arithmetic, cross_stack(): cross = jnp.stack([real_part, imag_part], 1).astype(jnp.bfloat16)  19.6 us
  transfers between devices with their start and end apart: 9, of which 8 were waited for; matrix products, arithmetic and copies ran while one was open for 17% of the time, Pallas kernels for 0%

commit v1 on v0

v1 whole, which is shorter than its diff:
```python
import math

import jax
import jax.numpy as jnp
from jax import lax
from jax.experimental import pallas as pl
from jax.experimental.pallas import tpu as pltpu
from jax.sharding import PartitionSpec as P

F = 4096
NB = 64
PAIRS = 2048
CHUNK = 256
CHUNKS = PAIRS // CHUNK
F32 = jnp.float32
BF16 = jnp.bfloat16
VMEM = pl.BlockSpec(memory_space=pltpu.VMEM)
SMEM = pl.BlockSpec(memory_space=pltpu.SMEM)


def shape(dims, dtype):
    return jax.ShapeDtypeStruct(dims, dtype)


def cost(flops, moved):
    return pl.CostEstimate(flops=flops, bytes_accessed=moved, transcendentals=0)


def split(x):
    hi = x.astype(BF16)
    return hi, (x - hi.astype(F32)).astype(BF16)


def power_kernel(x_ref, out_ref):
    x = x_ref[...].astype(F32)
    part = jnp.sum(x * x, axis=0, keepdims=True)
    out_ref[...] = jnp.broadcast_to(part[None], out_ref.shape)


def factors_kernel(me_ref, owner_row_ref, owner_col_ref, part_ref, hi_ref, lo_ref, select_ref):
    n = 128
    j = lax.broadcasted_iota(jnp.int32, (n, n), 0)
    i = lax.broadcasted_iota(jnp.int32, (n, n), 1)
    unit = 2.0 * math.pi / F
    first = ((i * (me_ref[0] * n + j)) % F).astype(F32) * unit
    step = ((n * j) % F).astype(F32) * unit
    re, im = jnp.cos(first), jnp.sin(first)
    sr, si = jnp.cos(step), jnp.sin(step)
    for block in range(F // n):
        lanes = pl.ds(block * n, n)
        hi, lo = split(re)
        hi_ref[:n, lanes] = hi
        lo_ref[:n, lanes] = lo
        hi, lo = split(-im)
        hi_ref[n:, lanes] = hi
        lo_ref[n:, lanes] = lo
        re, im = re * sr - im * si, re * si + im * sr
    row, col = owner_row_ref[...], owner_col_ref[...]
    b2 = lax.broadcasted_iota(jnp.int32, (NB, NB), 0)
    b = lax.broadcasted_iota(jnp.int32, (NB, NB), 1)
    ahead = jnp.where((col == row) & (b2 < b), 1.0, 0.0)
    rank = jnp.sum(ahead, axis=0, keepdims=True)
    slots = select_ref.shape[0]
    slot = row.astype(F32) * (slots // 8) + rank
    place = lax.broadcasted_iota(jnp.int32, (slots, NB), 0).astype(F32)
    select_ref[...] = jnp.where(place == slot, 1.0, 0.0).astype(BF16)


def white_kernel(parts_ref, x_ref, lists_ref, own_ref, *sent):
    power = jnp.sum(parts_ref[...], axis=0)
    rms = jnp.sqrt(power / (2 * F) + 1e-06)
    white = (x_ref[...].astype(F32) / rms).astype(BF16)
    own_ref[...] = white
    for k, ref in enumerate(sent):
        ref[:256, :] = white
        ref[256:, :] = lists_ref[k]


def add_list(index_ref, base, left_ref, right_ref, cross_ref, onehot_ref):
    def body(c, carry):
        rows = lax.broadcasted_iota(jnp.int32, (256, CHUNK), 0).astype(F32)
        bins = lax.broadcasted_iota(jnp.int32, (NB, CHUNK), 0).astype(F32)
        u = index_ref[pl.ds(base + c, 1), :]
        v = index_ref[pl.ds(base + CHUNKS + c, 1), :]
        b = index_ref[pl.ds(base + 2 * CHUNKS + c, 1), :]
        take_u = jnp.where(rows == u, 1.0, 0.0).astype(BF16)
        take_v = jnp.where(rows == v, 1.0, 0.0).astype(BF16)
        left = jnp.dot(left_ref[:256, :], take_u, preferred_element_type=F32)
        right = jnp.dot(right_ref[:256, :], take_v, preferred_element_type=F32)
        lr, li, rr, ri = left[:128], left[128:], right[:128], right[128:]
        lanes = pl.ds(pl.multiple_of(c * CHUNK, CHUNK), CHUNK)
        cross_ref[:128, lanes] = (lr * rr + li * ri).astype(BF16)
        cross_ref[128:, lanes] = (li * rr - lr * ri).astype(BF16)
        onehot_ref[:, lanes] = jnp.where(bins == b, 1.0, 0.0).astype(BF16)
        return carry

    lax.fori_loop(0, CHUNKS, body, 0)
    return lax.dot_general(
        onehot_ref[...], cross_ref[...], (((1,), (1,)), ((), ())), preferred_element_type=F32
    )


def pair_kernel(kind, *refs):
    if kind == "own":
        own_ref, lists_ref, out_ref, cross_ref, onehot_ref, index_ref = refs
        index_ref[:32, :] = lists_ref[...].astype(F32)
        out_ref[...] = add_list(index_ref, 0, own_ref, own_ref, cross_ref, onehot_ref)
    elif kind == "two":
        acc_ref, own_ref, lists_ref, got_ref, out_ref, cross_ref, onehot_ref, index_ref = refs
        index_ref[:32, :] = lists_ref[...].astype(F32)
        index_ref[32:, :] = got_ref[256:, :].astype(F32)
        out = acc_ref[...] + add_list(index_ref, 0, own_ref, got_ref, cross_ref, onehot_ref)
        out_ref[...] = out + add_list(index_ref, 32, got_ref, own_ref, cross_ref, onehot_ref)
    else:
        acc_ref, own_ref, lists_ref, got_ref, select_ref, out_ref, cross_ref, onehot_ref, index_ref = refs
        index_ref[:32, :] = lists_ref[...].astype(F32)
        acc = acc_ref[...] + add_list(index_ref, 0, own_ref, got_ref, cross_ref, onehot_ref)
        hi, lo = split(acc)
        pick = select_ref[...]
        owned = jnp.dot(pick, hi, preferred_element_type=F32) + jnp.dot(
            pick, lo, preferred_element_type=F32
        )
        out_ref[...] = owned.reshape(out_ref.shape)


def pair_call(kind, out_shape, *args):
    lists = 2 if kind == "two" else 1
    return pl.pallas_call(
        lambda *refs: pair_kernel(kind, *refs),
        out_shape=out_shape,
        in_specs=[VMEM] * len(args),
        out_specs=VMEM,
        scratch_shapes=[
            pltpu.VMEM((256, PAIRS), BF16),
            pltpu.VMEM((NB, PAIRS), BF16),
            pltpu.VMEM((64, CHUNK), F32),
        ],
        cost_estimate=cost(lists * 600_000_000, 1_000_000),
    )(*args)


def lag_kernel(got_ref, hi_ref, lo_ref, out_ref):
    owned = jnp.sum(got_ref[...], axis=0)
    rows = owned.shape[0]
    hi, lo = split(owned)
    both = jnp.concatenate([hi, lo], axis=0)
    for block in range(4):
        lanes = pl.ds(block * 1024, 1024)
        main = jnp.dot(both, hi_ref[:, lanes], preferred_element_type=F32)
        line = main[:rows] + main[rows:] + jnp.dot(hi, lo_ref[:, lanes], preferred_element_type=F32)
        for k in range(8):
            out_ref[block * 8 + k] = line[:, k * 128 : (k + 1) * 128].astype(out_ref.dtype)


def finish_kernel(scale, got_ref, out_ref):
    line = jnp.sum(got_ref[...].astype(F32), axis=0) * scale
    out_ref[...] = line.T


def on_device(spectra, pair_first, pair_second, pair_bin, bin_owner):
    blocks = lax.axis_size("blk")
    peers = lax.axis_size("freq")
    sensors, _, freq_dev = spectra.shape
    slots_each = 2 * NB // blocks
    scale = (F * PAIRS * blocks * blocks / NB) ** (-0.5)

    turned = jnp.transpose(spectra, (1, 2, 0)).reshape(2 * freq_dev, sensors)
    part = pl.pallas_call(
        power_kernel,
        out_shape=shape((peers, 1, sensors), F32),
        in_specs=[VMEM],
        out_specs=VMEM,
        cost_estimate=cost(200_000, 160_000),
    )(turned)
    parts = lax.all_to_all(part, "freq", 0, 0, tiled=True)

    me = lax.axis_index("freq").astype(jnp.int32).reshape(1)
    hi, lo, select = pl.pallas_call(
        factors_kernel,
        out_shape=(
            shape((2 * freq_dev, F), BF16),
            shape((2 * freq_dev, F), BF16),
            shape((2 * NB, NB), BF16),
        ),
        in_specs=[SMEM, VMEM, VMEM, pl.BlockSpec(memory_space=pl.ANY)],
        out_specs=[VMEM] * 3,
        cost_estimate=cost(10_000_000, 8_000_000),
    )(me, bin_owner.reshape(1, NB), bin_owner.reshape(NB, 1), part)

    listed = jnp.stack([pair_first[0], pair_second[0], pair_bin[0]], axis=1)
    listed = listed.reshape(blocks, 3 * CHUNKS, CHUNK).astype(BF16)
    listed = jnp.pad(listed, ((0, 0), (0, 8), (0, 0)))
    travelling = listed[blocks - 1 : blocks // 2 : -1]

    padded = 2 * freq_dev + 32
    own, *sent = pl.pallas_call(
        white_kernel,
        out_shape=[shape((2 * freq_dev, sensors), BF16)] + [shape((padded, sensors), BF16)] * 3,
        in_specs=[VMEM] * 3,
        out_specs=[VMEM] * 4,
        cost_estimate=cost(1_000_000, 800_000),
    )(parts, turned, travelling)

    def ahead(x, by):
        return lax.ppermute(x, "blk", [(i, (i + by) % blocks) for i in range(blocks)])

    got = [ahead(sent[k - 1] if k < 4 else own, k) for k in range(1, 5)]

    acc_shape = shape((NB, 2 * freq_dev), F32)
    acc = pair_call("own", acc_shape, own, listed[0])
    for k in (1, 2, 3):
        acc = pair_call("two", acc_shape, acc, own, listed[k], got[k - 1])
    stacks = pair_call(
        "last", shape((blocks, slots_each, 2 * freq_dev), F32), acc, own, listed[4], got[3], select
    )
    stacks = lax.all_to_all(stacks, "blk", 0, 0, tiled=True)

    line = pl.pallas_call(
        lag_kernel,
        out_shape=shape((peers, slots_each, freq_dev), BF16),
        in_specs=[VMEM] * 3,
        out_specs=VMEM,
        cost_estimate=cost(100_000_000, 4_500_000),
    )(stacks, hi, lo)
    line = lax.all_to_all(line, "freq", 0, 0, tiled=True)
    return pl.pallas_call(
        lambda *refs: finish_kernel(scale, *refs),
        out_shape=shape((freq_dev, slots_each), F32),
        in_specs=[VMEM],
        out_specs=VMEM,
        cost_estimate=cost(100_000, 150_000),
    )(line)


def solution(mesh):
    return jax.shard_map(
        on_device,
        mesh=mesh,
        in_specs=(
            P("blk", None, "freq"),
            P("blk", None, None),
            P("blk", None, None),
            P("blk", None, None),
            P(),
        ),
        out_specs=P("freq", "blk"),
        check_vma=False,
    )
```

time: 534 us -> 103 us (0.19); the launches traced: 524 us -> 102 us
  waiting for transfers between devices: 213 us -> 1.6 us
  local copies, waits for them, and re-layouts: 119 us -> 9.27 us
  other arithmetic: 70.4 us -> 1.74 us
  blocking collectives: 72.8 us -> 30.7 us
  Pallas kernels: 0 us -> 40.5 us
  matrix products: 28.5 us -> 0 us
  between operations: 14.4 us -> 0.06 us
  starting transfers between devices: 5.91 us -> 17.7 us
    gather x16 -> x0, local copies, waits for them, and re-layouts: 113 us -> none  [the longest x8 56.8 us: cross_stack(): right = remote[second_rows].astype(jnp.float32)]
    reduce_scatter x1 -> x0, waiting for transfers between devices: 111 us -> none  [on_device(): lax.psum_scatter(lag_block(lag_rows, freq_rows, owned), 'freq', scatter_d...]
    psum x1 -> x0, blocking collectives: 72.8 us -> none  [on_device(): power = lax.psum(jnp.sum(values * values, axis=(1, 2)), 'freq')]
    psum x1 -> x0, waiting for transfers between devices: 72.4 us -> none  [on_device(): totals = lax.psum(partial_stack, 'blk')]
    another operation x16 -> x3, other arithmetic: 46 us -> 1.74 us  [on_device(): listed = jnp.stack([pair_first[0], pair_second[0], pair_bin[0]], axis=1)]
    pallas_call x0 -> x10, Pallas kernels: none -> 40.5 us  [the longest x5 27.2 us: pair_call(): pl.pallas_call(lambda *refs: pair_kernel(kind, *refs), out_shape=out_shap...]
    all_to_all x0 -> x2, blocking collectives: none -> 30.7 us  [the longest x1 20.3 us: on_device(): line = lax.all_to_all(line, 'freq', 0, 0, tiled=True)]
    ppermute x7 -> x4, waiting for transfers between devices: 29.6 us -> 0.01 us  [ahead(): lax.ppermute(x, 'blk', [(i, (i + by) % blocks) for i in range(blocks)])]
  transfers between devices with their start and end apart: 9 -> 5, of which waited for: 8 -> 1; matrix products, arithmetic and copies ran while one was open for 17% -> 5% of each run, Pallas kernels for 0% -> 27%
where the time goes in v1:
time: 103 us; the launch traced here: 102 us
  Pallas kernels  40.5 us (39%)
  blocking collectives  30.7 us (30%)
  starting transfers between devices  17.7 us (17%)
  local copies, waits for them, and re-layouts  9.27 us (9%)
  other arithmetic  1.74 us (2%)
  waiting for transfers between devices  1.6 us (2%)
    pallas_call x5, Pallas kernels, pair_call(): pl.pallas_call(lambda *refs: pair_kernel(kind, *refs), out_shape=out_shap...  27.2 us
    all_to_all x1, blocking collectives, on_device(): line = lax.all_to_all(line, 'freq', 0, 0, tiled=True)  20.3 us
    all_to_all x1, starting transfers between devices, on_device(): parts = lax.all_to_all(part, 'freq', 0, 0, tiled=True)  11.3 us
    all_to_all x1, blocking collectives, on_device(): stacks = lax.all_to_all(stacks, 'blk', 0, 0, tiled=True)  10.4 us
    ppermute x4, starting transfers between devices, ahead(): lax.ppermute(x, 'blk', [(i, (i + by) % blocks) for i in range(blocks)])  6.39 us
    pallas_call x1, Pallas kernels, on_device(): pl.pallas_call(factors_kernel, out_shape=(shape((2 * freq_dev, F), BF16),...  4.57 us
    pallas_call x1, Pallas kernels, on_device(): pl.pallas_call(lag_kernel, out_shape=shape((peers, slots_each, freq_dev),...  3.64 us
    unnamed x10, local copies, waits for them, and re-layouts  3.26 us
  transfers between devices with their start and end apart: 5, of which 1 were waited for; matrix products, arithmetic and copies ran while one was open for 5% of the time, Pallas kernels for 27%

profile of v1, /device:TPU:8, one launch (start us, length us, event | category | flops | bytes accessed | tf_op | source)
XLA Modules:
  0.0 101.5 jit_solution(803102162706565609)
XLA Ops:
  0.0 1.7 %copy.10 = bf16[2,128,256]{2,1,0:T(8,128)(2,1)} copy(bf16[2,128,256]{1,0,2:T(2,128)(2,1)} %bitcast.23) | data formatting | bytes 262144 | tf_op jit(solution)/shard_map/transpose | solution.py:167
  1.7 1.6 %shard_map.55.part_ref = f32[32,1,256]{2,1,0:T(1,128)} custom-call(bf16[256,256]{1,0:T(8,128)(2,1)} %bitcast.21), custom_call_target="tpu_custom_call" | custom-call | flops 200000 | bytes 160000 | tf_op jit(solution)/shard_map/pallas_call | solution.py:168
  3.2 11.3 %all-to-all-start = ((f32[32,1,256]{2,1,0:T(1,128)}), f32[32,1,256]{2,1,0:T(1,128)S(1)}, u32[]{:S(2)}, u32[]{:S(2)}) async-start(f32[32,1,256]{2,1,0:T(1,128)} %shard_map.55.part_ref), calls=%async_computation | async-start | bytes 65536 | tf_op jit(solution)/shard_map/all_to_all | solution.py:175
  14.5 0.8 convert_bitcast_fusion.2
  15.4 1.3 %copy.12.owner_col_ref = s32[64,1]{1,0:T(8,128)} copy(s32[64,1]{0,1:T(1,128)} %bitcast.24) | data formatting | bytes 512 | tf_op jit(solution)/shard_map/reshape | solution.py:188
  16.7 0.9 convert_bitcast_fusion
  18.5 4.6 %shard_map.61 = (bf16[256,4096]{1,0:T(8,128)(2,1)}, bf16[256,4096]{1,0:T(8,128)(2,1)}, bf16[128,64]{1,0:T(8,128)(2,1)}) custom-call(s32[1]{0:T(128)} %bitcast.10.me_ref, s32[1,64]{1,0:T(1,128)} %bitcast.25, s32[64,1]{1,0:T(8,128)} %copy.12.owner_col_ref, f32[32,1,256]{2,1,0:T(1,128)} %shard_map.55.part_ref), custom_call_target="tpu_custom_call" | custom-call | flops 10000000 | bytes 8000000 | tf_op jit(solution)/shard_map/pallas_call | solution.py:178
  23.1 1.6 %all-to-all-done.parts_ref = f32[32,1,256]{2,1,0:T(1,128)S(1)} async-done(((f32[32,1,256]{2,1,0:T(1,128)}), f32[32,1,256]{2,1,0:T(1,128)S(1)}, u32[]{:S(2)}, u32[]{:S(2)}) %all-to-all-start) | async-done | bytes 32800 | tf_op jit(solution)/shard_map/all_to_all | solution.py:175
  25.3 1.8 %shard_map.56 = (bf16[256,256]{1,0:T(8,128)(2,1)}, bf16[288,256]{1,0:T(8,128)(2,1)}, bf16[288,256]{1,0:T(8,128)(2,1)}, bf16[288,256]{1,0:T(8,128)(2,1)}) custom-call(f32[32,1,256]{2,1,0:T(1,128)} %copy-done, bf16[256,256]{1,0:T(8,128)(2,1)} %bitcast.22, bf16[3,32,256]{2,1,0:T(8,128)(2,1)} %rev.3.lists_ref), custom_call_target="tpu_custom_call" | custom-call | flops 1000000 | bytes 800000 | tf_op jit(solution)/shard_map/pallas_call | solution.py:196
  27.1 1.6 %collective-permute-start = (bf16[288,256]{1,0:T(8,128)(2,1)}, bf16[288,256]{1,0:T(8,128)(2,1)S(1)}, u32[]{:S(2)}, u32[]{:S(2)}) collective-permute-start(bf16[288,256]{1,0:T(8,128)(2,1)} %get-tuple-element.13), channel_id=1, source_target_pairs={{0,32},{32,64},{64,96},{96,128},{128,160},{160,192},{192,224},{224... | collective-permute-start | bytes 442376 | tf_op jit(solution)/shard_map/ppermute | solution.py:205
  29.9 1.8 %collective-permute-start.1 = (bf16[288,256]{1,0:T(8,128)(2,1)}, bf16[288,256]{1,0:T(8,128)(2,1)S(1)}, u32[]{:S(2)}, u32[]{:S(2)}) collective-permute-start(bf16[288,256]{1,0:T(8,128)(2,1)} %get-tuple-element.14), channel_id=1, source_target_pairs={{0,64},{32,96},{64,128},{96,160},{128,192},{160,224},{192,0},{224,... | collective-permute-start | bytes 442376 | tf_op jit(solution)/shard_map/ppermute | solution.py:205
  31.7 2.4 %collective-permute-start.2 = (bf16[288,256]{1,0:T(8,128)(2,1)}, bf16[288,256]{1,0:T(8,128)(2,1)S(1)}, u32[]{:S(2)}, u32[]{:S(2)}) collective-permute-start(bf16[288,256]{1,0:T(8,128)(2,1)} %get-tuple-element.15), channel_id=1, source_target_pairs={{0,96},{32,128},{64,160},{96,192},{128,224},{160,0},{192,32},{224,... | collective-permute-start | bytes 442376 | tf_op jit(solution)/shard_map/ppermute | solution.py:205
  34.1 3.9 %shard_map.57.refs_0_ = f32[64,256]{1,0:T(8,128)} custom-call(bf16[256,256]{1,0:T(8,128)(2,1)} %get-tuple-element.12.refs_0_.refs_1_, bf16[32,256]{1,0:T(8,128)(2,1)} %get-tuple-element.20.refs_1_), custom_call_target="tpu_custom_call" | custom-call | flops 600000000 | bytes 1000000 | tf_op jit(solution)/shard_map/pallas_call | solution.py:128
  38.0 0.7 copy-done.1
  38.7 6.4 %shard_map.58.refs_0_ = f32[64,256]{1,0:T(8,128)} custom-call(f32[64,256]{1,0:T(8,128)} %shard_map.57.refs_0_, bf16[256,256]{1,0:T(8,128)(2,1)} %get-tuple-element.12.refs_0_.refs_1_, bf16[32,256]{1,0:T(8,128)(2,1)} %get-tuple-element.21.refs_2_, bf16[288,256]{1,0:T(8,128)(2,1)} %copy-done.1), custom_call_target="tpu_custom_call" | custom-call | flops 1200000000 | bytes 1000000 | tf_op jit(solution)/shard_map/pallas_call | solution.py:128
  45.7 6.4 %shard_map.59.refs_0_ = f32[64,256]{1,0:T(8,128)} custom-call(f32[64,256]{1,0:T(8,128)} %shard_map.58.refs_0_, bf16[256,256]{1,0:T(8,128)(2,1)} %get-tuple-element.12.refs_0_.refs_1_, bf16[32,256]{1,0:T(8,128)(2,1)} %get-tuple-element.22.refs_2_, bf16[288,256]{1,0:T(8,128)(2,1)} %copy-done.3), custom_call_target="tpu_custom_call" | custom-call | flops 1200000000 | bytes 1000000 | tf_op jit(solution)/shard_map/pallas_call | solution.py:128
  52.7 6.4 %shard_map.60.refs_0_ = f32[64,256]{1,0:T(8,128)} custom-call(f32[64,256]{1,0:T(8,128)} %shard_map.59.refs_0_, bf16[256,256]{1,0:T(8,128)(2,1)} %get-tuple-element.12.refs_0_.refs_1_, bf16[32,256]{1,0:T(8,128)(2,1)} %get-tuple-element.23.refs_2_, bf16[288,256]{1,0:T(8,128)(2,1)} %copy-done.2), custom_call_target="tpu_custom_call" | custom-call | flops 1200000000 | bytes 1000000 | tf_op jit(solution)/shard_map/pallas_call | solution.py:128
  59.1 0.7 copy-done.4
  59.8 4.3 %shard_map.62 = f32[8,16,256]{2,1,0:T(8,128)} custom-call(f32[64,256]{1,0:T(8,128)} %shard_map.60.refs_0_, bf16[256,256]{1,0:T(8,128)(2,1)} %get-tuple-element.12.refs_0_.refs_1_, bf16[32,256]{1,0:T(8,128)(2,1)} %get-tuple-element.19.refs_2_, bf16[256,256]{1,0:T(8,128)(2,1)} %copy-done.4, bf16[128,64]{1,0:T(8,128)(2,1)} %get-tuple-element.16.refs_4_), custom_call_target="tpu_custom_call" | custom-call | flops 600000000 | bytes 1000000 | tf_op jit(solution)/shard_map/pallas_call | solution.py:128
  64.0 10.4 %all_to_all.15.got_ref = f32[8,16,256]{2,1,0:T(8,128)} all-to-all(f32[8,16,256]{2,1,0:T(8,128)} %shard_map.62), channel_id=1, replica_groups=mesh['blk'=8,'freq'=32] {'blk'}, dimensions={0} | all-to-all | bytes 262144 | tf_op jit(solution)/shard_map/all_to_all | solution.py:216
  74.4 3.6 %shard_map.63 = bf16[32,16,128]{2,1,0:T(8,128)(2,1)} custom-call(f32[8,16,256]{2,1,0:T(8,128)} %all_to_all.15.got_ref, bf16[256,4096]{1,0:T(8,128)(2,1)} %get-tuple-element.17.hi_ref, bf16[256,4096]{1,0:T(8,128)(2,1)} %get-tuple-element.18.lo_ref), custom_call_target="tpu_custom_call" | custom-call | flops 100000000 | bytes 4500000 | tf_op jit(solution)/shard_map/pallas_call | solution.py:218
  78.1 20.3 %all_to_all.16.refs_0_ = bf16[32,16,128]{2,1,0:T(8,128)(2,1)} all-to-all(bf16[32,16,128]{2,1,0:T(8,128)(2,1)} %shard_map.63), channel_id=1, replica_groups=mesh['blk'=8,'freq'=32] {'freq'}, dimensions={0} | all-to-all | bytes 262144 | tf_op jit(solution)/shard_map/all_to_all | solution.py:225
  98.3 1.7 %shard_map.64 = f32[128,16]{1,0:T(8,128)} custom-call(bf16[32,16,128]{2,1,0:T(8,128)(2,1)} %all_to_all.16.refs_0_), custom_call_target="tpu_custom_call" | custom-call | flops 100000 | bytes 150000 | tf_op jit(solution)/shard_map/pallas_call | solution.py:226
  100.0 1.5 %copy.13 = f32[128,16]{0,1:T(8,128)} copy(f32[128,16]{1,0:T(8,128)} %shard_map.64) | data formatting | bytes 16384 | tf_op jit(solution)/shard_map/pallas_call | solution.py:226
  (19 shorter events, 4.0 us)
Async XLA Ops:
  3.2 21.4 %all-to-all-start = ((f32[32,1,256]{2,1,0:T(1,128)}), f32[32,1,256]{2,1,0:T(1,128)S(1)}, u32[]{:S(2)}, u32[]{:S(2)}) async-start(f32[32,1,256]{2,1,0:T(1,128)} %shard_map.55.part_ref), calls=%async_computation | async-start | bytes 65536 | tf_op jit(solution)/shard_map/all_to_all | solution.py:175
  24.6 0.6 copy-start
  27.1 10.9 %collective-permute-start = (bf16[288,256]{1,0:T(8,128)(2,1)}, bf16[288,256]{1,0:T(8,128)(2,1)S(1)}, u32[]{:S(2)}, u32[]{:S(2)}) collective-permute-start(bf16[288,256]{1,0:T(8,128)(2,1)} %get-tuple-element.13), channel_id=1, source_target_pairs={{0,32},{32,64},{64,96},{96,128},{128,160},{160,192},{192,224},{224... | collective-permute-start | bytes 442376 | tf_op jit(solution)/shard_map/ppermute | solution.py:205
  29.3 29.8 %collective-permute-start.3 = (bf16[256,256]{1,0:T(8,128)(2,1)}, bf16[256,256]{1,0:T(8,128)(2,1)S(1)}, u32[]{:S(2)}, u32[]{:S(2)}) collective-permute-start(bf16[256,256]{1,0:T(8,128)(2,1)} %get-tuple-element.12.refs_0_.refs_1_), channel_id=1, source_target_pairs={{0,128},{32,160},{64,192},{96,224},{128,0},{160,32},{192,64},{224,... | collective-permute-start | bytes 393224 | tf_op jit(solution)/shard_map/ppermute | solution.py:205
  29.9 15.1 %collective-permute-start.1 = (bf16[288,256]{1,0:T(8,128)(2,1)}, bf16[288,256]{1,0:T(8,128)(2,1)S(1)}, u32[]{:S(2)}, u32[]{:S(2)}) collective-permute-start(bf16[288,256]{1,0:T(8,128)(2,1)} %get-tuple-element.14), channel_id=1, source_target_pairs={{0,64},{32,96},{64,128},{96,160},{128,192},{160,224},{192,0},{224,... | collective-permute-start | bytes 442376 | tf_op jit(solution)/shard_map/ppermute | solution.py:205
  31.7 20.4 %collective-permute-start.2 = (bf16[288,256]{1,0:T(8,128)(2,1)}, bf16[288,256]{1,0:T(8,128)(2,1)S(1)}, u32[]{:S(2)}, u32[]{:S(2)}) collective-permute-start(bf16[288,256]{1,0:T(8,128)(2,1)} %get-tuple-element.15), channel_id=1, source_target_pairs={{0,96},{32,128},{64,160},{96,192},{128,224},{160,0},{192,32},{224,... | collective-permute-start | bytes 442376 | tf_op jit(solution)/shard_map/ppermute | solution.py:205
  38.0 0.7 copy-start.1
  45.1 0.7 copy-start.3
  52.1 0.7 copy-start.2
  59.1 0.7 copy-start.4

commit v2 on v0

v2 whole, which is shorter than its diff:
```python
import functools
import math

import jax
import jax.numpy as jnp
from jax import lax
from jax.experimental import pallas as pl
from jax.experimental.pallas import tpu as pltpu
from jax.sharding import PartitionSpec as P

F = 4096
NB = 64
PAIRS = 2048
CHUNK = 256
CHUNKS = PAIRS // CHUNK
F32 = jnp.float32
BF16 = jnp.bfloat16
VMEM = pl.BlockSpec(memory_space=pltpu.VMEM)
SMEM = pl.BlockSpec(memory_space=pltpu.SMEM)


def shape(dims, dtype):
    return jax.ShapeDtypeStruct(dims, dtype)


def call(kernel, out_shape, args, mib, flops, moved, specs=None, scratch=()):
    return pl.pallas_call(
        kernel,
        out_shape=out_shape,
        in_specs=[VMEM] * len(args) if specs is None else specs,
        out_specs=jax.tree.map(lambda _: VMEM, out_shape),
        scratch_shapes=list(scratch),
        compiler_params=pltpu.CompilerParams(vmem_limit_bytes=None if mib is None else mib << 20),
        cost_estimate=pl.CostEstimate(flops=flops, bytes_accessed=moved, transcendentals=0),
    )(*args)


def split(x):
    hi = x.astype(BF16)
    return hi, (x - hi.astype(F32)).astype(BF16)


def power_kernel(x_ref, part_ref, flat_ref):
    re, im = x_ref[:, 0, :], x_ref[:, 1, :]
    flat_ref[:, :128] = re
    flat_ref[:, 128:] = im
    re, im = re.astype(F32), im.astype(F32)
    hi, lo = split(re * re + im * im)
    ones = jnp.full((8, 128), 1.0, BF16)
    dims = (((1,), (1,)), ((), ()))
    part = lax.dot_general(ones, hi, dims, preferred_element_type=F32)
    part = part + lax.dot_general(ones, lo, dims, preferred_element_type=F32)
    part_ref[...] = jnp.broadcast_to(part[None, :1], part_ref.shape)


def list_rows(lists, r):
    rows = [
        ref[0, r : r + 1, c * CHUNK : (c + 1) * CHUNK] for ref in lists for c in range(CHUNKS)
    ]
    rows = jnp.concatenate(rows, axis=0).astype(F32)
    return jnp.concatenate([rows, jnp.zeros((CHUNKS, CHUNK), F32)], axis=0)


def factors_kernel(
    me_ref, owner_ref, first_ref, second_ref, bin_ref, part_ref, out_ref, select_ref, rows_ref
):
    for r in range(rows_ref.shape[0]):
        rows_ref[r] = list_rows((first_ref, second_ref, bin_ref), r).astype(BF16)
    n = 128
    j = lax.broadcasted_iota(jnp.int32, (n, n), 0)
    i = lax.broadcasted_iota(jnp.int32, (n, n), 1)
    unit = 2.0 * math.pi / F
    first = ((i * (me_ref[0] * n + j)) & (F - 1)).astype(F32) * unit
    step = ((n * j) & (F - 1)).astype(F32) * unit
    re, im = jnp.cos(first), jnp.sin(first)
    sr, si = jnp.cos(step), jnp.sin(step)
    for block in range(F // n):
        lanes = pl.ds(block * n, n)
        out_ref[:n, lanes] = re.astype(BF16)
        out_ref[n:, lanes] = (-im).astype(BF16)
        re, im = re * sr - im * si, re * si + im * sr
    row = jnp.broadcast_to(owner_ref[...].astype(F32), (NB, NB))
    b2 = lax.broadcasted_iota(jnp.int32, (NB, NB), 0)
    b = lax.broadcasted_iota(jnp.int32, (NB, NB), 1)
    ahead = jnp.where((row.T == row) & (b2 < b), 1.0, 0.0)
    rank = jnp.sum(ahead, axis=0, keepdims=True)
    slots = select_ref.shape[0]
    slot = row[:1] * (slots // 8) + rank
    place = lax.broadcasted_iota(jnp.int32, (slots, NB), 0).astype(F32)
    select_ref[...] = jnp.where(place == slot, 1.0, 0.0).astype(BF16)


def white_kernel(parts_ref, x_ref, rows_ref, own_ref, *sent):
    power = jnp.sum(parts_ref[...], axis=0)
    rms = jnp.sqrt(power / (2 * F) + 1e-06)
    rms = jnp.broadcast_to(rms, (8, 256)).T[:, :1]
    white = (x_ref[...].astype(F32) / rms).astype(BF16)
    own_ref[...] = white
    for k, ref in enumerate(sent):
        ref[:256, :] = white
        ref[256:, :] = rows_ref[7 - k]


def column_onehot(col):
    lanes = lax.broadcasted_iota(jnp.int32, (CHUNK, 256), 1).astype(F32).astype(BF16)
    same = lanes == jnp.broadcast_to(col, (CHUNK, 256))
    return jnp.where(same, jnp.asarray(1.0, BF16), jnp.asarray(0.0, BF16))


def add_list(rows, left_block, right_block):
    index = rows[: 2 * CHUNKS].T.astype(BF16)
    take_u = [column_onehot(index[:, c : c + 1]) for c in range(CHUNKS)]
    take_v = [column_onehot(index[:, CHUNKS + c : CHUNKS + c + 1]) for c in range(CHUNKS)]
    left = jnp.dot(jnp.concatenate(take_u, 0), left_block, preferred_element_type=F32)
    right = jnp.dot(jnp.concatenate(take_v, 0), right_block, preferred_element_type=F32)
    lr, li, rr, ri = left[:, :128], left[:, 128:], right[:, :128], right[:, 128:]
    re = (lr * rr + li * ri).astype(BF16)
    im = (li * rr - lr * ri).astype(BF16)
    cross = jnp.concatenate([re, im], axis=1)
    bins = lax.broadcasted_iota(jnp.int32, (NB, CHUNK), 0).astype(F32)
    onehot = [
        jnp.where(bins == rows[2 * CHUNKS + c : 2 * CHUNKS + c + 1], 1.0, 0.0).astype(BF16)
        for c in range(CHUNKS)
    ]
    return jnp.dot(jnp.concatenate(onehot, 1), cross, preferred_element_type=F32)


def pair_kernel(steps, first, last, *refs):
    refs = list(refs)
    acc = None if first else refs.pop(0)[...]
    own_ref, rows_ref = refs[:2]
    got = refs[2 : 2 + len(steps)]
    out_ref = refs[-1]
    if first:
        acc = add_list(rows_ref[0].astype(F32), own_ref[...], own_ref[...])
    for k, got_ref in zip(steps, got):
        acc = acc + add_list(rows_ref[k].astype(F32), own_ref[...], got_ref[:256, :])
        if k < 4:
            acc = acc + add_list(got_ref[256:, :].astype(F32), got_ref[:256, :], own_ref[...])
    if last:
        pick = refs[2 + len(steps)][...]
        owned = jnp.dot(pick, acc.astype(BF16), preferred_element_type=F32)
        acc = owned.reshape(out_ref.shape)
    out_ref[...] = acc.astype(out_ref.dtype)


def pair_call(steps, out_shape, acc, own, lists, got, select):
    first, last = acc is None, select is not None
    args = [] if first else [acc]
    args += [own, lists, *got]
    args += [select] if last else []
    kernel = functools.partial(pair_kernel, steps, first, last)
    return call(kernel, out_shape, args, 20, 1_200_000_000 * max(len(steps), 1), 1_000_000)


def lag_kernel(got_ref, factors_ref, out_ref):
    owned = jnp.sum(got_ref[...].astype(F32), axis=0)
    rows = owned.shape[0]
    both = jnp.concatenate(split(owned), axis=0)
    for block in range(4):
        lanes = pl.ds(block * 1024, 1024)
        line = jnp.dot(both, factors_ref[:, lanes], preferred_element_type=F32)
        line = line[:rows] + line[rows:]
        for k in range(8):
            out_ref[block * 8 + k] = line[:, k * 128 : (k + 1) * 128].astype(out_ref.dtype)


def finish_kernel(scale, got_ref, out_ref):
    out_ref[...] = jnp.sum(got_ref[...].astype(F32), axis=0) * scale


def on_device(spectra, pair_first, pair_second, pair_bin, bin_owner):
    blocks = lax.axis_size("blk")
    peers = lax.axis_size("freq")
    sensors, _, freq_dev = spectra.shape
    width = 2 * freq_dev
    slots_each = 2 * NB // blocks
    scale = (F * PAIRS * blocks * blocks / NB) ** (-0.5)
    lists = (pair_first, pair_second, pair_bin)

    part, flat = call(
        power_kernel,
        [shape((peers, 1, sensors), F32), shape((sensors, width), BF16)],
        (spectra,), None, 1_000_000, 300_000,
    )
    parts = lax.all_to_all(part, "freq", 0, 0, tiled=True)

    me = lax.axis_index("freq").astype(jnp.int32).reshape(1)
    factors, select, rows = call(
        factors_kernel,
        [
            shape((width, F), BF16),
            shape((2 * NB, NB), BF16),
            shape((blocks, 4 * CHUNKS, CHUNK), BF16),
        ],
        (me, bin_owner.reshape(1, NB), *lists, part), 8, 10_000_000, 8_000_000,
        specs=[SMEM] + [VMEM] * 4 + [pl.BlockSpec(memory_space=pl.ANY)],
    )

    own, *sent = call(
        white_kernel,
        [shape((sensors, width), BF16)] + [shape((sensors + 32, width), BF16)] * 3,
        (parts, flat, rows), 4, 1_000_000, 800_000,
    )

    def ahead(x, by):
        return lax.ppermute(x, "blk", [(i, (i + by) % blocks) for i in range(blocks)])

    got = {k: ahead(sent[k - 1] if k < 4 else own, k) for k in (2, 1, 3, 4)}

    acc_shape = shape((NB, width), F32)
    acc = pair_call((), acc_shape, None, own, rows, (), None)
    acc = pair_call((1, 3), acc_shape, acc, own, rows, (got[1], got[3]), None)
    stacks = pair_call(
        (2, 4), shape((blocks, slots_each, width), BF16), acc, own, rows, (got[2], got[4]), select
    )
    stacks = lax.all_to_all(stacks, "blk", 0, 0, tiled=True)

    line = call(
        lag_kernel, shape((peers, slots_each, freq_dev), BF16), (stacks, factors), 6, 100_000_000, 2_500_000
    )
    line = lax.all_to_all(line, "freq", 0, 0, tiled=True)
    out = call(
        functools.partial(finish_kernel, scale), shape((slots_each, freq_dev), F32), (line,), 2, 100_000, 150_000
    )
    return out.T


def solution(mesh):
    return jax.shard_map(
        on_device,
        mesh=mesh,
        in_specs=(
            P("blk", None, "freq"),
            P("blk", None, None),
            P("blk", None, None),
            P("blk", None, None),
            P(),
        ),
        out_specs=P("freq", "blk"),
        check_vma=False,
    )
```

time: 534 us -> 73.2 us (0.14); the launches traced: 524 us -> 71.9 us
  waiting for transfers between devices: 213 us -> 9.98 us
  local copies, waits for them, and re-layouts: 119 us -> 4.86 us
  other arithmetic: 70.4 us -> 0 us
  blocking collectives: 72.8 us -> 26.1 us
  matrix products: 28.5 us -> 0 us
  between operations: 14.4 us -> 0.09 us
  Pallas kernels: 0 us -> 13.7 us
  starting transfers between devices: 5.91 us -> 17.2 us
    gather x16 -> x0, local copies, waits for them, and re-layouts: 113 us -> none  [the longest x8 56.8 us: cross_stack(): right = remote[second_rows].astype(jnp.float32)]
    reduce_scatter x1 -> x0, waiting for transfers between devices: 111 us -> none  [on_device(): lax.psum_scatter(lag_block(lag_rows, freq_rows, owned), 'freq', scatter_d...]
    psum x1 -> x0, blocking collectives: 72.8 us -> none  [on_device(): power = lax.psum(jnp.sum(values * values, axis=(1, 2)), 'freq')]
    psum x1 -> x0, waiting for transfers between devices: 72.4 us -> none  [on_device(): totals = lax.psum(partial_stack, 'blk')]
    another operation x16 -> x0, other arithmetic: 46 us -> none
    dot_general x11 -> x0, matrix products: 28.5 us -> none  [the longest x1 11.2 us: lag_block(): jnp.dot(jnp.sin(phase), piece[:, 1, :].T, precision=lax.Precision.HIGHEST)]
    all_to_all x0 -> x2, blocking collectives: none -> 26.1 us  [the longest x1 18.1 us: on_device(): line = lax.all_to_all(line, 'freq', 0, 0, tiled=True)]
    ppermute x7 -> x4, waiting for transfers between devices: 29.6 us -> 5.4 us  [ahead(): lax.ppermute(x, 'blk', [(i, (i + by) % blocks) for i in range(blocks)])]
  transfers between devices with their start and end apart: 9 -> 5, of which waited for: 8 -> 3; matrix products, arithmetic and copies ran while one was open for 17% -> 0% of each run, Pallas kernels for 0% -> 9%
where the time goes in v2:
time: 73.2 us; the launch traced here: 71.9 us
  blocking collectives  26.1 us (36%)
  starting transfers between devices  17.2 us (23%)
  Pallas kernels  13.7 us (19%)
  waiting for transfers between devices  9.98 us (14%)
  local copies, waits for them, and re-layouts  4.86 us (7%)
    all_to_all x1, blocking collectives, on_device(): line = lax.all_to_all(line, 'freq', 0, 0, tiled=True)  18.1 us
    pallas_call x8, Pallas kernels, call(): pl.pallas_call(kernel, out_shape=out_shape, in_specs=[VMEM] * len(args) i...  13.7 us
    all_to_all x1, starting transfers between devices, on_device(): parts = lax.all_to_all(part, 'freq', 0, 0, tiled=True)  11.3 us
    all_to_all x1, blocking collectives, on_device(): stacks = lax.all_to_all(stacks, 'blk', 0, 0, tiled=True)  8.05 us
    ppermute x4, starting transfers between devices, ahead(): lax.ppermute(x, 'blk', [(i, (i + by) % blocks) for i in range(blocks)])  5.86 us
    ppermute x4, waiting for transfers between devices, ahead(): lax.ppermute(x, 'blk', [(i, (i + by) % blocks) for i in range(blocks)])  5.4 us
    unnamed x12, local copies, waits for them, and re-layouts  4.86 us
    all_to_all x1, waiting for transfers between devices, on_device(): parts = lax.all_to_all(part, 'freq', 0, 0, tiled=True)  4.58 us
  transfers between devices with their start and end apart: 5, of which 3 were waited for; matrix products, arithmetic and copies ran while one was open for 0% of the time, Pallas kernels for 9%

profile of v2, /device:TPU:8, one launch (start us, length us, event | category | flops | bytes accessed | tf_op | source)
XLA Modules:
  0.0 71.9 jit_solution(18146711860301121269)
XLA Ops:
  0.0 2.8 %shard_map.55 = (f32[32,1,256]{2,1,0:T(1,128)}, bf16[256,256]{1,0:T(8,128)(2,1)}) custom-call(bf16[256,2,128]{2,1,0:T(2,128)(2,1)} %x_ref.1), custom_call_target="tpu_custom_call" | custom-call | flops 1000000 | bytes 300000 | tf_op jit(solution)/shard_map/pallas_call | solution.py:27
  2.8 11.3 %all-to-all-start = ((f32[32,1,256]{2,1,0:T(1,128)}), f32[32,1,256]{2,1,0:T(1,128)S(1)}, u32[]{:S(2)}, u32[]{:S(2)}) async-start(f32[32,1,256]{2,1,0:T(1,128)} %get-tuple-element.14.part_ref), calls=%async_computation | async-start | bytes 65536 | tf_op jit(solution)/shard_map/all_to_all | solution.py:186
  14.1 0.8 %copy-done = f32[32,1,256]{2,1,0:T(1,128)S(1)} copy-done((f32[32,1,256]{2,1,0:T(1,128)S(1)}, f32[32,1,256]{2,1,0:T(1,128)}, u32[]{:S(2)}) %copy-start) | copy-done | bytes 32792
  14.9 0.8 %copy-done.2 = s32[1,8,2048]{2,1,0:T(8,128)S(1)} copy-done((s32[1,8,2048]{2,1,0:T(8,128)S(1)}, s32[1,8,2048]{2,1,0:T(8,128)}, u32[]{:S(2)}) %copy-start.2) | copy-done | bytes 65560
  15.8 0.8 %copy-done.3 = s32[1,8,2048]{2,1,0:T(8,128)S(1)} copy-done((s32[1,8,2048]{2,1,0:T(8,128)S(1)}, s32[1,8,2048]{2,1,0:T(8,128)}, u32[]{:S(2)}) %copy-start.3) | copy-done | bytes 65560
  16.6 0.8 %copy-done.4 = s32[1,8,2048]{2,1,0:T(8,128)S(1)} copy-done((s32[1,8,2048]{2,1,0:T(8,128)S(1)}, s32[1,8,2048]{2,1,0:T(8,128)}, u32[]{:S(2)}) %copy-start.4) | copy-done | bytes 65560
  17.5 0.7 copy-done.5
  18.1 1.5 %shard_map.56 = (bf16[256,4096]{1,0:T(8,128)(2,1)S(1)}, bf16[128,64]{1,0:T(8,128)(2,1)S(1)}, bf16[8,32,256]{2,1,0:T(8,128)(2,1)S(1)}) custom-call(s32[1]{0:T(128)} %bitcast.me_ref, s32[1,64]{1,0:T(1,128)S(1)} %bitcast.3, s32[1,8,2048]{2,1,0:T(8,128)S(1)} %copy-done.2, s32[1,8,2048]{2,1,0:T(8,128)S(1)} %copy-done.3, s32[1,8,2048]{2,1,0:T(8,128)S(1)} %copy-done.4, ...), custom_call_target="tpu_custom_call" | custom-call | flops 10000000 | bytes 8000000 | tf_op jit(solution)/shard_map/pallas_call | solution.py:27
  19.7 4.6 %all-to-all-done.parts_ref = f32[32,1,256]{2,1,0:T(1,128)S(1)} async-done(((f32[32,1,256]{2,1,0:T(1,128)}), f32[32,1,256]{2,1,0:T(1,128)S(1)}, u32[]{:S(2)}, u32[]{:S(2)}) %all-to-all-start) | async-done | bytes 32800 | tf_op jit(solution)/shard_map/all_to_all | solution.py:186
  24.2 0.9 %copy-done.1 = bf16[256,256]{1,0:T(8,128)(2,1)S(1)} copy-done((bf16[256,256]{1,0:T(8,128)(2,1)S(1)}, bf16[256,256]{1,0:T(8,128)(2,1)}, u32[]{:S(2)}) %copy-start.1) | copy-done | bytes 131096
  25.1 0.3 shard_map.57
  25.5 1.7 %collective-permute-start = (bf16[288,256]{1,0:T(8,128)(2,1)S(1)}, bf16[288,256]{1,0:T(8,128)(2,1)S(1)}, u32[]{:S(2)}, u32[]{:S(2)}) collective-permute-start(bf16[288,256]{1,0:T(8,128)(2,1)S(1)} %get-tuple-element.18), channel_id=1, source_target_pairs={{0,32},{32,64},{64,96},{96,128},{128,160},{160,192},{192,224},{224... | collective-permute-start | bytes 442376 | tf_op jit(solution)/shard_map/ppermute | solution.py:207
  27.1 0.5 collective-permute-start.1
  27.6 1.4 %collective-permute-start.3 = (bf16[256,256]{1,0:T(8,128)(2,1)S(1)}, bf16[256,256]{1,0:T(8,128)(2,1)S(1)}, u32[]{:S(2)}, u32[]{:S(2)}) collective-permute-start(bf16[256,256]{1,0:T(8,128)(2,1)S(1)} %get-tuple-element.17.refs_0_.refs_1_), channel_id=1, source_target_pairs={{0,128},{32,160},{64,192},{96,224},{128,0},{160,32},{192,64},{224,... | collective-permute-start | bytes 393224 | tf_op jit(solution)/shard_map/ppermute | solution.py:207
  29.0 2.3 %collective-permute-start.2 = (bf16[288,256]{1,0:T(8,128)(2,1)S(1)}, bf16[288,256]{1,0:T(8,128)(2,1)S(1)}, u32[]{:S(2)}, u32[]{:S(2)}) collective-permute-start(bf16[288,256]{1,0:T(8,128)(2,1)S(1)} %get-tuple-element.20), channel_id=1, source_target_pairs={{0,64},{32,96},{64,128},{96,160},{128,192},{160,224},{192,0},{224,... | collective-permute-start | bytes 442376 | tf_op jit(solution)/shard_map/ppermute | solution.py:207
  31.3 1.1 %shard_map.58.refs_0_ = f32[64,256]{1,0:T(8,128)S(1)} custom-call(bf16[256,256]{1,0:T(8,128)(2,1)S(1)} %get-tuple-element.17.refs_0_.refs_1_, bf16[8,32,256]{2,1,0:T(8,128)(2,1)S(1)} %get-tuple-element.16.rows_ref.refs_1_.refs_2_), custom_call_target="tpu_custom_call" | custom-call | flops 1200000000 | bytes 1000000 | tf_op jit(solution)/shard_map/pallas_call | solution.py:27
  32.4 2.3 %collective-permute-done.1.refs_4_ = bf16[288,256]{1,0:T(8,128)(2,1)S(1)} collective-permute-done((bf16[288,256]{1,0:T(8,128)(2,1)S(1)}, bf16[288,256]{1,0:T(8,128)(2,1)S(1)}, u32[]{:S(2)}, u32[]{:S(2)}) %collective-permute-start.1) | collective-permute-done | bytes 147488 | tf_op jit(solution)/shard_map/ppermute | solution.py:207
  34.7 3.6 %shard_map.59.refs_0_ = f32[64,256]{1,0:T(8,128)S(1)} custom-call(f32[64,256]{1,0:T(8,128)S(1)} %shard_map.58.refs_0_, bf16[256,256]{1,0:T(8,128)(2,1)S(1)} %get-tuple-element.17.refs_0_.refs_1_, bf16[8,32,256]{2,1,0:T(8,128)(2,1)S(1)} %get-tuple-element.16.rows_ref.refs_1_.refs_2_, bf16[288,256]{1,0:T(8,128)(2,1)S(1)} %collective-permute-done.refs_3_, ...), custom_call_target="tpu_custom_call" | custom-call | flops 2400000000 | bytes 1000000 | tf_op jit(solution)/shard_map/pallas_call | solution.py:27
  38.3 3.1 %collective-permute-done.2.refs_3_ = bf16[288,256]{1,0:T(8,128)(2,1)S(1)} collective-permute-done((bf16[288,256]{1,0:T(8,128)(2,1)S(1)}, bf16[288,256]{1,0:T(8,128)(2,1)S(1)}, u32[]{:S(2)}, u32[]{:S(2)}) %collective-permute-start.2) | collective-permute-done | bytes 147488 | tf_op jit(solution)/shard_map/ppermute | solution.py:207
  41.4 3.3 %shard_map.60 = bf16[8,16,256]{2,1,0:T(8,128)(2,1)S(1)} custom-call(f32[64,256]{1,0:T(8,128)S(1)} %shard_map.59.refs_0_, bf16[256,256]{1,0:T(8,128)(2,1)S(1)} %get-tuple-element.17.refs_0_.refs_1_, bf16[8,32,256]{2,1,0:T(8,128)(2,1)S(1)} %get-tuple-element.16.rows_ref.refs_1_.refs_2_, bf16[288,256]{1,0:T(8,128)(2,1)S(1)} %collective-permute-done.2.refs_3_, ...), custom_call_target="tpu_custom_call" | custom-call | flops 2400000000 | bytes 1000000 | tf_op jit(solution)/shard_map/pallas_call | solution.py:27
  44.7 8.1 %all_to_all.15.got_ref = bf16[8,16,256]{2,1,0:T(8,128)(2,1)S(1)} all-to-all(bf16[8,16,256]{2,1,0:T(8,128)(2,1)S(1)} %shard_map.60), channel_id=1, replica_groups=mesh['blk'=8,'freq'=32] {'blk'}, dimensions={0} | all-to-all | bytes 131072 | tf_op jit(solution)/shard_map/all_to_all | solution.py:217
  52.8 0.4 shard_map.61
  53.2 18.1 %all_to_all.16.got_ref = bf16[32,16,128]{2,1,0:T(8,128)(2,1)S(1)} all-to-all(bf16[32,16,128]{2,1,0:T(8,128)(2,1)S(1)} %shard_map.61), channel_id=1, replica_groups=mesh['blk'=8,'freq'=32] {'freq'}, dimensions={0} | all-to-all | bytes 262144 | tf_op jit(solution)/shard_map/all_to_all | solution.py:222
  71.3 0.6 shard_map.62
  (8 shorter events, 0.0 us)
Async XLA Ops:
  2.8 21.4 %all-to-all-start = ((f32[32,1,256]{2,1,0:T(1,128)}), f32[32,1,256]{2,1,0:T(1,128)S(1)}, u32[]{:S(2)}, u32[]{:S(2)}) async-start(f32[32,1,256]{2,1,0:T(1,128)} %get-tuple-element.14.part_ref), calls=%async_computation | async-start | bytes 65536 | tf_op jit(solution)/shard_map/all_to_all | solution.py:186
  14.1 0.8 %copy-start = (f32[32,1,256]{2,1,0:T(1,128)S(1)}, f32[32,1,256]{2,1,0:T(1,128)}, u32[]{:S(2)}) copy-start(f32[32,1,256]{2,1,0:T(1,128)} %get-tuple-element.14.part_ref) | copy-start | bytes 98308
  14.9 0.8 %copy-start.2 = (s32[1,8,2048]{2,1,0:T(8,128)S(1)}, s32[1,8,2048]{2,1,0:T(8,128)}, u32[]{:S(2)}) copy-start(s32[1,8,2048]{2,1,0:T(8,128)} %first_ref.1) | copy-start | bytes 196612
  15.8 0.8 %copy-start.3 = (s32[1,8,2048]{2,1,0:T(8,128)S(1)}, s32[1,8,2048]{2,1,0:T(8,128)}, u32[]{:S(2)}) copy-start(s32[1,8,2048]{2,1,0:T(8,128)} %second_ref.1) | copy-start | bytes 196612
  16.6 0.8 %copy-start.4 = (s32[1,8,2048]{2,1,0:T(8,128)S(1)}, s32[1,8,2048]{2,1,0:T(8,128)}, u32[]{:S(2)}) copy-start(s32[1,8,2048]{2,1,0:T(8,128)} %bin_ref.1) | copy-start | bytes 196612
  17.5 0.7 copy-start.5
  24.2 0.9 %copy-start.1 = (bf16[256,256]{1,0:T(8,128)(2,1)S(1)}, bf16[256,256]{1,0:T(8,128)(2,1)}, u32[]{:S(2)}) copy-start(bf16[256,256]{1,0:T(8,128)(2,1)} %get-tuple-element.15.x_ref) | copy-start | bytes 393220
  25.5 7.0 %collective-permute-start = (bf16[288,256]{1,0:T(8,128)(2,1)S(1)}, bf16[288,256]{1,0:T(8,128)(2,1)S(1)}, u32[]{:S(2)}, u32[]{:S(2)}) collective-permute-start(bf16[288,256]{1,0:T(8,128)(2,1)S(1)} %get-tuple-element.18), channel_id=1, source_target_pairs={{0,32},{32,64},{64,96},{96,128},{128,160},{160,192},{192,224},{224... | collective-permute-start | bytes 442376 | tf_op jit(solution)/shard_map/ppermute | solution.py:207
  27.1 7.6 %collective-permute-start.1 = (bf16[288,256]{1,0:T(8,128)(2,1)S(1)}, bf16[288,256]{1,0:T(8,128)(2,1)S(1)}, u32[]{:S(2)}, u32[]{:S(2)}) collective-permute-start(bf16[288,256]{1,0:T(8,128)(2,1)S(1)} %get-tuple-element.19), channel_id=1, source_target_pairs={{0,96},{32,128},{64,160},{96,192},{128,224},{160,0},{192,32},{224,... | collective-permute-start | bytes 442376 | tf_op jit(solution)/shard_map/ppermute | solution.py:207
  27.6 10.7 %collective-permute-start.3 = (bf16[256,256]{1,0:T(8,128)(2,1)S(1)}, bf16[256,256]{1,0:T(8,128)(2,1)S(1)}, u32[]{:S(2)}, u32[]{:S(2)}) collective-permute-start(bf16[256,256]{1,0:T(8,128)(2,1)S(1)} %get-tuple-element.17.refs_0_.refs_1_), channel_id=1, source_target_pairs={{0,128},{32,160},{64,192},{96,224},{128,0},{160,32},{192,64},{224,... | collective-permute-start | bytes 393224 | tf_op jit(solution)/shard_map/ppermute | solution.py:207
  29.0 12.4 %collective-permute-start.2 = (bf16[288,256]{1,0:T(8,128)(2,1)S(1)}, bf16[288,256]{1,0:T(8,128)(2,1)S(1)}, u32[]{:S(2)}, u32[]{:S(2)}) collective-permute-start(bf16[288,256]{1,0:T(8,128)(2,1)S(1)} %get-tuple-element.20), channel_id=1, source_target_pairs={{0,64},{32,96},{64,128},{96,160},{128,192},{160,224},{192,0},{224,... | collective-permute-start | bytes 442376 | tf_op jit(solution)/shard_map/ppermute | solution.py:207

commit v3 on v2

--- a/solution.py
+++ b/solution.py
@@ -7,6 +7,7 @@
 from jax.experimental import pallas as pl
 from jax.experimental.pallas import tpu as pltpu
 from jax.sharding import PartitionSpec as P
+
 
 F = 4096
 NB = 64
@@ -40,11 +41,12 @@
     return hi, (x - hi.astype(F32)).astype(BF16)
 
 
-def power_kernel(x_ref, part_ref, flat_ref):
-    re, im = x_ref[:, 0, :], x_ref[:, 1, :]
-    flat_ref[:, :128] = re
-    flat_ref[:, 128:] = im
-    re, im = re.astype(F32), im.astype(F32)
+def power_kernel(x_ref, part_ref, flat_ref, wide_ref):
+    wide_ref[...] = x_ref[...].astype(F32)
+    re = wide_ref[pl.ds(0, 256, stride=2), :]
+    im = wide_ref[pl.ds(1, 256, stride=2), :]
+    flat_ref[:, :128] = re.astype(BF16)
+    flat_ref[:, 128:] = im.astype(BF16)
     hi, lo = split(re * re + im * im)
     ones = jnp.full((8, 128), 1.0, BF16)
     dims = (((1,), (1,)), ((), ()))
@@ -61,11 +63,12 @@
     return jnp.concatenate([rows, jnp.zeros((CHUNKS, CHUNK), F32)], axis=0)
 
 
-def factors_kernel(
-    me_ref, owner_ref, first_ref, second_ref, bin_ref, part_ref, out_ref, select_ref, rows_ref
-):
+def rows_kernel(first_ref, second_ref, bin_ref, part_ref, rows_ref):
     for r in range(rows_ref.shape[0]):
         rows_ref[r] = list_rows((first_ref, second_ref, bin_ref), r).astype(BF16)
+
+
+def factors_kernel(me_ref, owner_ref, after_ref, out_ref, select_ref):
     n = 128
     j = lax.broadcasted_iota(jnp.int32, (n, n), 0)
     i = lax.broadcasted_iota(jnp.int32, (n, n), 1)
@@ -181,20 +184,15 @@
     part, flat = call(
         power_kernel,
         [shape((peers, 1, sensors), F32), shape((sensors, width), BF16)],
-        (spectra,), None, 1_000_000, 300_000,
+        (spectra.reshape(2 * sensors, freq_dev),), 4, 1_000_000, 300_000,
+        scratch=[pltpu.VMEM((2 * sensors, freq_dev), F32)],
     )
     parts = lax.all_to_all(part, "freq", 0, 0, tiled=True)
 
-    me = lax.axis_index("freq").astype(jnp.int32).reshape(1)
-    factors, select, rows = call(
-        factors_kernel,
-        [
-            shape((width, F), BF16),
-            shape((2 * NB, NB), BF16),
-            shape((blocks, 4 * CHUNKS, CHUNK), BF16),
-        ],
-        (me, bin_owner.reshape(1, NB), *lists, part), 8, 10_000_000, 8_000_000,
-        specs=[SMEM] + [VMEM] * 4 + [pl.BlockSpec(memory_space=pl.ANY)],
+    anywhere = pl.BlockSpec(memory_space=pl.ANY)
+    rows = call(
+        rows_kernel, shape((blocks, 4 * CHUNKS, CHUNK), BF16), (*lists, part), 4, 1_000_000, 400_000,
+        specs=[VMEM] * 3 + [anywhere],
     )
 
     own, *sent = call(
@@ -206,14 +204,20 @@
     def ahead(x, by):
         return lax.ppermute(x, "blk", [(i, (i + by) % blocks) for i in range(blocks)])
 
-    got = {k: ahead(sent[k - 1] if k < 4 else own, k) for k in (2, 1, 3, 4)}
+    got = {k: ahead(sent[k - 1] if k < 4 else own, k) for k in (2, 4, 1, 3)}
 
     acc_shape = shape((NB, width), F32)
     acc = pair_call((), acc_shape, None, own, rows, (), None)
-    acc = pair_call((1, 3), acc_shape, acc, own, rows, (got[1], got[3]), None)
-    stacks = pair_call(
-        (2, 4), shape((blocks, slots_each, width), BF16), acc, own, rows, (got[2], got[4]), select
-    )
+    for k in (4, 1, 3):
+        acc = pair_call((k,), acc_shape, acc, own, rows, (got[k],), None)
+    me = lax.axis_index("freq").astype(jnp.int32).reshape(1)
+    factors, select = call(
+        factors_kernel, [shape((width, F), BF16), shape((2 * NB, NB), BF16)],
+        (me, bin_owner.reshape(1, NB), acc), 8, 10_000_000, 8_000_000,
+        specs=[SMEM, VMEM, anywhere],
+    )
+    stacks_shape = shape((blocks, slots_each, width), BF16)
+    stacks = pair_call((2,), stacks_shape, acc, own, rows, (got[2],), select)
     stacks = lax.all_to_all(stacks, "blk", 0, 0, tiled=True)
 
     line = call(

time: 73.2 us -> 69.7 us (0.952)
  local copies, waits for them, and re-layouts: 4.86 us -> 3.42 us
  Pallas kernels: 13.7 us -> 12.5 us
    all_to_all x1, blocking collectives: 18.1 us -> 14.9 us  [on_device(): line = lax.all_to_all(line, 'freq', 0, 0, tiled=True)]
    ppermute x4, waiting for transfers between devices: 5.4 us -> 2.33 us  [ahead(): lax.ppermute(x, 'blk', [(i, (i + by) % blocks) for i in range(blocks)])]
    all_to_all x1, waiting for transfers between devices: 4.58 us -> 7.49 us  [on_device(): parts = lax.all_to_all(part, 'freq', 0, 0, tiled=True)]
    all_to_all x1, blocking collectives: 8.05 us -> 10.5 us  [on_device(): stacks = lax.all_to_all(stacks, 'blk', 0, 0, tiled=True)]
    unnamed x12 -> x10, local copies, waits for them, and re-layouts: 4.86 us -> 3.42 us
    pallas_call x8 -> x11, Pallas kernels: 13.7 us -> 12.5 us  [call(): pl.pallas_call(kernel, out_shape=out_shape, in_specs=[VMEM] * len(args) i...]
  transfers between devices with their start and end apart: 5 -> 5, of which waited for: 3 -> 3; matrix products, arithmetic and copies ran while one was open for 0% -> 0% of each run, Pallas kernels for 9% -> 12%
where the time goes in v3:
time: 69.7 us; the launch traced here: 68.5 us
  blocking collectives  25.4 us (36%)
  starting transfers between devices  17.3 us (25%)
  Pallas kernels  12.5 us (18%)
  waiting for transfers between devices  9.82 us (14%)
  local copies, waits for them, and re-layouts  3.42 us (5%)
    all_to_all x1, blocking collectives, on_device(): line = lax.all_to_all(line, 'freq', 0, 0, tiled=True)  14.9 us
    pallas_call x11, Pallas kernels, call(): pl.pallas_call(kernel, out_shape=out_shape, in_specs=[VMEM] * len(args) i...  12.5 us
    all_to_all x1, starting transfers between devices, on_device(): parts = lax.all_to_all(part, 'freq', 0, 0, tiled=True)  11.3 us
    all_to_all x1, blocking collectives, on_device(): stacks = lax.all_to_all(stacks, 'blk', 0, 0, tiled=True)  10.5 us
    all_to_all x1, waiting for transfers between devices, on_device(): parts = lax.all_to_all(part, 'freq', 0, 0, tiled=True)  7.49 us
    ppermute x4, starting transfers between devices, ahead(): lax.ppermute(x, 'blk', [(i, (i + by) % blocks) for i in range(blocks)])  5.95 us
    unnamed x10, local copies, waits for them, and re-layouts  3.42 us
    ppermute x4, waiting for transfers between devices, ahead(): lax.ppermute(x, 'blk', [(i, (i + by) % blocks) for i in range(blocks)])  2.33 us
  transfers between devices with their start and end apart: 5, of which 3 were waited for; matrix products, arithmetic and copies ran while one was open for 0% of the time, Pallas kernels for 12%

profile of v3, /device:TPU:8, one launch (start us, length us, event | category | flops | bytes accessed | tf_op | source)
XLA Modules:
  0.0 68.5 jit_solution(1388170451043955268)
XLA Ops:
  0.0 0.9 %copy-done = bf16[256,2,128]{2,1,0:T(2,128)(2,1)S(1)} copy-done((bf16[256,2,128]{2,1,0:T(2,128)(2,1)S(1)}, bf16[256,2,128]{2,1,0:T(2,128)(2,1)}, u32[]{:S(2)}) %copy-start) | copy-done | bytes 131096
  0.9 0.8 %shard_map.55 = (f32[32,1,256]{2,1,0:T(1,128)}, bf16[256,256]{1,0:T(8,128)(2,1)S(1)}) custom-call(bf16[512,128]{1,0:T(8,128)(2,1)S(1)} %bitcast.4), custom_call_target="tpu_custom_call" | custom-call | flops 1000000 | bytes 300000 | tf_op jit(solution)/shard_map/pallas_call | solution.py:28
  1.7 11.3 %all-to-all-start = ((f32[32,1,256]{2,1,0:T(1,128)}), f32[32,1,256]{2,1,0:T(1,128)S(1)}, u32[]{:S(2)}, u32[]{:S(2)}) async-start(f32[32,1,256]{2,1,0:T(1,128)} %get-tuple-element.13.part_ref), calls=%async_computation | async-start | bytes 65536 | tf_op jit(solution)/shard_map/all_to_all | solution.py:190
  13.0 0.8 %copy-done.1 = s32[1,8,2048]{2,1,0:T(8,128)S(1)} copy-done((s32[1,8,2048]{2,1,0:T(8,128)S(1)}, s32[1,8,2048]{2,1,0:T(8,128)}, u32[]{:S(2)}) %copy-start.1) | copy-done | bytes 65560
  13.9 0.8 %copy-done.2 = s32[1,8,2048]{2,1,0:T(8,128)S(1)} copy-done((s32[1,8,2048]{2,1,0:T(8,128)S(1)}, s32[1,8,2048]{2,1,0:T(8,128)}, u32[]{:S(2)}) %copy-start.2) | copy-done | bytes 65560
  14.7 0.8 %copy-done.3 = s32[1,8,2048]{2,1,0:T(8,128)S(1)} copy-done((s32[1,8,2048]{2,1,0:T(8,128)S(1)}, s32[1,8,2048]{2,1,0:T(8,128)}, u32[]{:S(2)}) %copy-start.3) | copy-done | bytes 65560
  15.6 7.5 %all-to-all-done.parts_ref = f32[32,1,256]{2,1,0:T(1,128)S(1)} async-done(((f32[32,1,256]{2,1,0:T(1,128)}), f32[32,1,256]{2,1,0:T(1,128)S(1)}, u32[]{:S(2)}, u32[]{:S(2)}) %all-to-all-start) | async-done | bytes 32800 | tf_op jit(solution)/shard_map/all_to_all | solution.py:190
  23.1 0.3 shard_map.57
  23.4 0.7 collective-permute-start
  24.1 1.6 %collective-permute-start.1 = (bf16[288,256]{1,0:T(8,128)(2,1)S(1)}, bf16[288,256]{1,0:T(8,128)(2,1)S(1)}, u32[]{:S(2)}, u32[]{:S(2)}) collective-permute-start(bf16[288,256]{1,0:T(8,128)(2,1)S(1)} %get-tuple-element.16), channel_id=1, source_target_pairs={{0,32},{32,64},{64,96},{96,128},{128,160},{160,192},{192,224},{224... | collective-permute-start | bytes 442376 | tf_op jit(solution)/shard_map/ppermute | solution.py:205
  25.7 1.1 %shard_map.58.refs_0_ = f32[64,256]{1,0:T(8,128)S(1)} custom-call(bf16[256,256]{1,0:T(8,128)(2,1)S(1)} %get-tuple-element.15.refs_0_.refs_1_, bf16[8,32,256]{2,1,0:T(8,128)(2,1)S(1)} %shard_map.56.rows_ref.refs_1_.refs_2_), custom_call_target="tpu_custom_call" | custom-call | flops 1200000000 | bytes 1000000 | tf_op jit(solution)/shard_map/pallas_call | solution.py:28
  26.8 1.4 %collective-permute-start.2 = (bf16[288,256]{1,0:T(8,128)(2,1)S(1)}, bf16[288,256]{1,0:T(8,128)(2,1)S(1)}, u32[]{:S(2)}, u32[]{:S(2)}) collective-permute-start(bf16[288,256]{1,0:T(8,128)(2,1)S(1)} %get-tuple-element.17), channel_id=1, source_target_pairs={{0,96},{32,128},{64,160},{96,192},{128,224},{160,0},{192,32},{224,... | collective-permute-start | bytes 442376 | tf_op jit(solution)/shard_map/ppermute | solution.py:205
  28.2 2.3 %collective-permute-start.3 = (bf16[288,256]{1,0:T(8,128)(2,1)S(1)}, bf16[288,256]{1,0:T(8,128)(2,1)S(1)}, u32[]{:S(2)}, u32[]{:S(2)}) collective-permute-start(bf16[288,256]{1,0:T(8,128)(2,1)S(1)} %get-tuple-element.18), channel_id=1, source_target_pairs={{0,64},{32,96},{64,128},{96,160},{128,192},{160,224},{192,0},{224,... | collective-permute-start | bytes 442376 | tf_op jit(solution)/shard_map/ppermute | solution.py:205
  30.5 1.1 %shard_map.59.refs_0_ = f32[64,256]{1,0:T(8,128)S(1)} custom-call(f32[64,256]{1,0:T(8,128)S(1)} %shard_map.58.refs_0_, bf16[256,256]{1,0:T(8,128)(2,1)S(1)} %get-tuple-element.15.refs_0_.refs_1_, bf16[8,32,256]{2,1,0:T(8,128)(2,1)S(1)} %shard_map.56.rows_ref.refs_1_.refs_2_, bf16[256,256]{1,0:T(8,128)(2,1)S(1)} %collective-permute-done.refs_3_), custom_call_target="tpu_custom_call" | custom-call | flops 1200000000 | bytes 1000000 | tf_op jit(solution)/shard_map/pallas_call | solution.py:28
  31.6 2.1 %shard_map.60.refs_0_ = f32[64,256]{1,0:T(8,128)S(1)} custom-call(f32[64,256]{1,0:T(8,128)S(1)} %shard_map.59.refs_0_, bf16[256,256]{1,0:T(8,128)(2,1)S(1)} %get-tuple-element.15.refs_0_.refs_1_, bf16[8,32,256]{2,1,0:T(8,128)(2,1)S(1)} %shard_map.56.rows_ref.refs_1_.refs_2_, bf16[288,256]{1,0:T(8,128)(2,1)S(1)} %collective-permute-done.1.refs_3_), custom_call_target="tpu_custom_call" | custom-call | flops 1200000000 | bytes 1000000 | tf_op jit(solution)/shard_map/pallas_call | solution.py:28
  33.8 0.5 collective-permute-done.2.refs_3_
  34.3 2.1 %shard_map.61.after_ref.refs_0_ = f32[64,256]{1,0:T(8,128)S(1)} custom-call(f32[64,256]{1,0:T(8,128)S(1)} %shard_map.60.refs_0_, bf16[256,256]{1,0:T(8,128)(2,1)S(1)} %get-tuple-element.15.refs_0_.refs_1_, bf16[8,32,256]{2,1,0:T(8,128)(2,1)S(1)} %shard_map.56.rows_ref.refs_1_.refs_2_, bf16[288,256]{1,0:T(8,128)(2,1)S(1)} %collective-permute-done.2.refs_3_), custom_call_target="tpu_custom_call" | custom-call | flops 1200000000 | bytes 1000000 | tf_op jit(solution)/shard_map/pallas_call | solution.py:28
  36.4 1.5 %shard_map.62 = (bf16[256,4096]{1,0:T(8,128)(2,1)S(1)}, bf16[128,64]{1,0:T(8,128)(2,1)S(1)}) custom-call(s32[1]{0:T(128)} %bitcast.1.me_ref, s32[1,64]{1,0:T(1,128)S(1)} %bitcast.5, f32[64,256]{1,0:T(8,128)S(1)} %shard_map.61.after_ref.refs_0_), custom_call_target="tpu_custom_call" | custom-call | flops 10000000 | bytes 8000000 | tf_op jit(solution)/shard_map/pallas_call | solution.py:28
  37.9 1.8 %collective-permute-done.3.refs_3_ = bf16[288,256]{1,0:T(8,128)(2,1)S(1)} collective-permute-done((bf16[288,256]{1,0:T(8,128)(2,1)S(1)}, bf16[288,256]{1,0:T(8,128)(2,1)S(1)}, u32[]{:S(2)}, u32[]{:S(2)}) %collective-permute-start.3) | collective-permute-done | bytes 147488 | tf_op jit(solution)/shard_map/ppermute | solution.py:205
  39.7 2.3 %shard_map.63 = bf16[8,16,256]{2,1,0:T(8,128)(2,1)S(1)} custom-call(f32[64,256]{1,0:T(8,128)S(1)} %shard_map.61.after_ref.refs_0_, bf16[256,256]{1,0:T(8,128)(2,1)S(1)} %get-tuple-element.15.refs_0_.refs_1_, bf16[8,32,256]{2,1,0:T(8,128)(2,1)S(1)} %shard_map.56.rows_ref.refs_1_.refs_2_, bf16[288,256]{1,0:T(8,128)(2,1)S(1)} %collective-permute-done.3.refs_3_, ...), custom_call_target="tpu_custom_call" | custom-call | flops 1200000000 | bytes 1000000 | tf_op jit(solution)/shard_map/pallas_call | solution.py:28
  42.0 10.5 %all_to_all.15.got_ref = bf16[8,16,256]{2,1,0:T(8,128)(2,1)S(1)} all-to-all(bf16[8,16,256]{2,1,0:T(8,128)(2,1)S(1)} %shard_map.63), channel_id=1, replica_groups=mesh['blk'=8,'freq'=32] {'blk'}, dimensions={0} | all-to-all | bytes 131072 | tf_op jit(solution)/shard_map/all_to_all | solution.py:221
  52.5 0.4 shard_map.64
  53.0 14.9 %all_to_all.16.got_ref = bf16[32,16,128]{2,1,0:T(8,128)(2,1)S(1)} all-to-all(bf16[32,16,128]{2,1,0:T(8,128)(2,1)S(1)} %shard_map.64), channel_id=1, replica_groups=mesh['blk'=8,'freq'=32] {'freq'}, dimensions={0} | all-to-all | bytes 262144 | tf_op jit(solution)/shard_map/all_to_all | solution.py:226
  67.9 0.6 shard_map.65
  (9 shorter events, 0.1 us)
Async XLA Ops:
  0.0 0.9 %copy-start = (bf16[256,2,128]{2,1,0:T(2,128)(2,1)S(1)}, bf16[256,2,128]{2,1,0:T(2,128)(2,1)}, u32[]{:S(2)}) copy-start(bf16[256,2,128]{2,1,0:T(2,128)(2,1)} %param.5) | copy-start | bytes 393220
  1.7 21.4 %all-to-all-start = ((f32[32,1,256]{2,1,0:T(1,128)}), f32[32,1,256]{2,1,0:T(1,128)S(1)}, u32[]{:S(2)}, u32[]{:S(2)}) async-start(f32[32,1,256]{2,1,0:T(1,128)} %get-tuple-element.13.part_ref), calls=%async_computation | async-start | bytes 65536 | tf_op jit(solution)/shard_map/all_to_all | solution.py:190
  13.0 0.8 %copy-start.1 = (s32[1,8,2048]{2,1,0:T(8,128)S(1)}, s32[1,8,2048]{2,1,0:T(8,128)}, u32[]{:S(2)}) copy-start(s32[1,8,2048]{2,1,0:T(8,128)} %first_ref.1) | copy-start | bytes 196612
  13.9 0.8 %copy-start.2 = (s32[1,8,2048]{2,1,0:T(8,128)S(1)}, s32[1,8,2048]{2,1,0:T(8,128)}, u32[]{:S(2)}) copy-start(s32[1,8,2048]{2,1,0:T(8,128)} %second_ref.1) | copy-start | bytes 196612
  14.7 0.8 %copy-start.3 = (s32[1,8,2048]{2,1,0:T(8,128)S(1)}, s32[1,8,2048]{2,1,0:T(8,128)}, u32[]{:S(2)}) copy-start(s32[1,8,2048]{2,1,0:T(8,128)} %bin_ref.1) | copy-start | bytes 196612
  23.4 7.1 %collective-permute-start = (bf16[256,256]{1,0:T(8,128)(2,1)S(1)}, bf16[256,256]{1,0:T(8,128)(2,1)S(1)}, u32[]{:S(2)}, u32[]{:S(2)}) collective-permute-start(bf16[256,256]{1,0:T(8,128)(2,1)S(1)} %get-tuple-element.15.refs_0_.refs_1_), channel_id=1, source_target_pairs={{0,128},{32,160},{64,192},{96,224},{128,0},{160,32},{192,64},{224,... | collective-permute-start | bytes 393224 | tf_op jit(solution)/shard_map/ppermute | solution.py:205
  24.1 7.5 %collective-permute-start.1 = (bf16[288,256]{1,0:T(8,128)(2,1)S(1)}, bf16[288,256]{1,0:T(8,128)(2,1)S(1)}, u32[]{:S(2)}, u32[]{:S(2)}) collective-permute-start(bf16[288,256]{1,0:T(8,128)(2,1)S(1)} %get-tuple-element.16), channel_id=1, source_target_pairs={{0,32},{32,64},{64,96},{96,128},{128,160},{160,192},{192,224},{224... | collective-permute-start | bytes 442376 | tf_op jit(solution)/shard_map/ppermute | solution.py:205
  26.8 7.5 %collective-permute-start.2 = (bf16[288,256]{1,0:T(8,128)(2,1)S(1)}, bf16[288,256]{1,0:T(8,128)(2,1)S(1)}, u32[]{:S(2)}, u32[]{:S(2)}) collective-permute-start(bf16[288,256]{1,0:T(8,128)(2,1)S(1)} %get-tuple-element.17), channel_id=1, source_target_pairs={{0,96},{32,128},{64,160},{96,192},{128,224},{160,0},{192,32},{224,... | collective-permute-start | bytes 442376 | tf_op jit(solution)/shard_map/ppermute | solution.py:205
  28.2 11.6 %collective-permute-start.3 = (bf16[288,256]{1,0:T(8,128)(2,1)S(1)}, bf16[288,256]{1,0:T(8,128)(2,1)S(1)}, u32[]{:S(2)}, u32[]{:S(2)}) collective-permute-start(bf16[288,256]{1,0:T(8,128)(2,1)S(1)} %get-tuple-element.18), channel_id=1, source_target_pairs={{0,64},{32,96},{64,128},{96,160},{128,192},{160,224},{192,0},{224,... | collective-permute-start | bytes 442376 | tf_op jit(solution)/shard_map/ppermute | solution.py:205
  33.7 2.7 %copy-start.4 = (s32[64]{0:T(128)S(1)}, s32[64]{0:T(128)}, u32[]{:S(2)}) copy-start(s32[64]{0:T(128)} %param.9) | copy-start | bytes 772

commit v4 on v3

--- a/solution.py
+++ b/solution.py
@@ -18,6 +18,29 @@
 BF16 = jnp.bfloat16
 VMEM = pl.BlockSpec(memory_space=pltpu.VMEM)
 SMEM = pl.BlockSpec(memory_space=pltpu.SMEM)
+
+
+def target(kind, a):
+    if kind == "beside":
+        return a - a % 4 + (a + 1) % 4
+    if kind == "corner":
+        return (a - a % 4 + 4) % 8 + (a + 3) % 4
+    if kind == "across":
+        return (a + 4) % 8
+    return (a + 2) % 8
+
+
+def source(kind, a):
+    if kind == "beside":
+        return a - a % 4 + (a + 3) % 4
+    if kind == "corner":
+        return (a - a % 4 + 4) % 8 + (a + 1) % 4
+    if kind == "across":
+        return (a + 4) % 8
+    return (a + 6) % 8
+
+
+TWO_WAY = ("beside", "corner", "far")
 
 
 def shape(dims, dtype):
@@ -63,12 +86,9 @@
     return jnp.concatenate([rows, jnp.zeros((CHUNKS, CHUNK), F32)], axis=0)
 
 
-def rows_kernel(first_ref, second_ref, bin_ref, part_ref, rows_ref):
+def factors_kernel(me_ref, first_ref, second_ref, bin_ref, part_ref, out_ref, rows_ref):
     for r in range(rows_ref.shape[0]):
         rows_ref[r] = list_rows((first_ref, second_ref, bin_ref), r).astype(BF16)
-
-
-def factors_kernel(me_ref, owner_ref, after_ref, out_ref, select_ref):
     n = 128
     j = lax.broadcasted_iota(jnp.int32, (n, n), 0)
     i = lax.broadcasted_iota(jnp.int32, (n, n), 1)
@@ -82,6 +102,9 @@
         out_ref[:n, lanes] = re.astype(BF16)
         out_ref[n:, lanes] = (-im).astype(BF16)
         re, im = re * sr - im * si, re * si + im * sr
+
+
+def select_kernel(owner_ref, after_ref, select_ref):
     row = jnp.broadcast_to(owner_ref[...].astype(F32), (NB, NB))
     b2 = lax.broadcasted_iota(jnp.int32, (NB, NB), 0)
     b = lax.broadcasted_iota(jnp.int32, (NB, NB), 1)
@@ -99,9 +122,10 @@
     rms = jnp.broadcast_to(rms, (8, 256)).T[:, :1]
     white = (x_ref[...].astype(F32) / rms).astype(BF16)
     own_ref[...] = white
-    for k, ref in enumerate(sent):
+    me = lax.axis_index("blk")
+    for kind, ref in zip(TWO_WAY, sent):
         ref[:256, :] = white
-        ref[256:, :] = rows_ref[7 - k]
+        ref[256:, :] = rows_ref[lax.rem(me - target(kind, me) + 8, 8)]
 
 
 def column_onehot(col):
@@ -128,32 +152,34 @@
     return jnp.dot(jnp.concatenate(onehot, 1), cross, preferred_element_type=F32)
 
 
-def pair_kernel(steps, first, last, *refs):
+def pair_kernel(kinds, first, last, *refs):
     refs = list(refs)
     acc = None if first else refs.pop(0)[...]
     own_ref, rows_ref = refs[:2]
-    got = refs[2 : 2 + len(steps)]
+    got = refs[2 : 2 + len(kinds)]
     out_ref = refs[-1]
     if first:
         acc = add_list(rows_ref[0].astype(F32), own_ref[...], own_ref[...])
-    for k, got_ref in zip(steps, got):
-        acc = acc + add_list(rows_ref[k].astype(F32), own_ref[...], got_ref[:256, :])
-        if k < 4:
+    me = lax.axis_index("blk")
+    for kind, got_ref in zip(kinds, got):
+        mine = rows_ref[lax.rem(me - source(kind, me) + 8, 8)].astype(F32)
+        acc = acc + add_list(mine, own_ref[...], got_ref[:256, :])
+        if kind in TWO_WAY:
             acc = acc + add_list(got_ref[256:, :].astype(F32), got_ref[:256, :], own_ref[...])
     if last:
-        pick = refs[2 + len(steps)][...]
+        pick = refs[2 + len(kinds)][...]
         owned = jnp.dot(pick, acc.astype(BF16), preferred_element_type=F32)
         acc = owned.reshape(out_ref.shape)
     out_ref[...] = acc.astype(out_ref.dtype)
 
 
-def pair_call(steps, out_shape, acc, own, lists, got, select):
+def pair_call(kinds, out_shape, acc, own, lists, got, select):
     first, last = acc is None, select is not None
     args = [] if first else [acc]
     args += [own, lists, *got]
     args += [select] if last else []
-    kernel = functools.partial(pair_kernel, steps, first, last)
-    return call(kernel, out_shape, args, 20, 1_200_000_000 * max(len(steps), 1), 1_000_000)
+    kernel = functools.partial(pair_kernel, kinds, first, last)
+    return call(kernel, out_shape, args, 20, 1_200_000_000 * max(len(kinds), 1), 1_000_000)
 
 
 def lag_kernel(got_ref, factors_ref, out_ref):
@@ -190,9 +216,12 @@
     parts = lax.all_to_all(part, "freq", 0, 0, tiled=True)
 
     anywhere = pl.BlockSpec(memory_space=pl.ANY)
-    rows = call(
-        rows_kernel, shape((blocks, 4 * CHUNKS, CHUNK), BF16), (*lists, part), 4, 1_000_000, 400_000,
-        specs=[VMEM] * 3 + [anywhere],
+    me = lax.axis_index("freq").astype(jnp.int32).reshape(1)
+    factors, rows = call(
+        factors_kernel,
+        [shape((width, F), BF16), shape((blocks, 4 * CHUNKS, CHUNK), BF16)],
+        (me, *lists, part), 8, 10_000_000, 8_000_000,
+        specs=[SMEM] + [VMEM] * 3 + [anywhere],
     )
 
     own, *sent = call(
@@ -201,23 +230,23 @@
         (parts, flat, rows), 4, 1_000_000, 800_000,
     )
 
-    def ahead(x, by):
-        return lax.ppermute(x, "blk", [(i, (i + by) % blocks) for i in range(blocks)])
-
-    got = {k: ahead(sent[k - 1] if k < 4 else own, k) for k in (2, 4, 1, 3)}
+    sent = dict(zip(TWO_WAY, sent), across=own)
+
+    def exchange(kind):
+        return lax.ppermute(sent[kind], "blk", [(a, target(kind, a)) for a in range(blocks)])
+
+    got = {kind: exchange(kind) for kind in ("far", "beside", "corner", "across")}
 
     acc_shape = shape((NB, width), F32)
     acc = pair_call((), acc_shape, None, own, rows, (), None)
-    for k in (4, 1, 3):
-        acc = pair_call((k,), acc_shape, acc, own, rows, (got[k],), None)
-    me = lax.axis_index("freq").astype(jnp.int32).reshape(1)
-    factors, select = call(
-        factors_kernel, [shape((width, F), BF16), shape((2 * NB, NB), BF16)],
-        (me, bin_owner.reshape(1, NB), acc), 8, 10_000_000, 8_000_000,
-        specs=[SMEM, VMEM, anywhere],
+    for kind in ("beside", "across", "corner"):
+        acc = pair_call((kind,), acc_shape, acc, own, rows, (got[kind],), None)
+    select = call(
+        select_kernel, shape((2 * NB, NB), BF16), (bin_owner.reshape(1, NB), acc), 2, 100_000, 30_000,
+        specs=[VMEM, anywhere],
     )
     stacks_shape = shape((blocks, slots_each, width), BF16)
-    stacks = pair_call((2,), stacks_shape, acc, own, rows, (got[2],), select)
+    stacks = pair_call(("far",), stacks_shape, acc, own, rows, (got["far"],), select)
     stacks = lax.all_to_all(stacks, "blk", 0, 0, tiled=True)
 
     line = call(

time: 69.7 us -> 66.9 us (0.960)
  waiting for transfers between devices: 9.82 us -> 8.08 us
  blocking collectives: 25.4 us -> 24.5 us
    all_to_all x1, blocking collectives: 10.5 us -> 8.73 us  [on_device(): stacks = lax.all_to_all(stacks, 'blk', 0, 0, tiled=True)]
    all_to_all x1, waiting for transfers between devices: 7.49 us -> 6.29 us  [on_device(): parts = lax.all_to_all(part, 'freq', 0, 0, tiled=True)]
    all_to_all x1, blocking collectives: 14.9 us -> 15.7 us  [on_device(): line = lax.all_to_all(line, 'freq', 0, 0, tiled=True)]
  transfers between devices with their start and end apart: 5 -> 5, of which waited for: 3 -> 2; matrix products, arithmetic and copies ran while one was open for 0% -> 0% of each run, Pallas kernels for 12% -> 12%
where the time goes in v4:
time: 66.9 us; the launch traced here: 65.8 us
  blocking collectives  24.5 us (37%)
  starting transfers between devices  17.3 us (26%)
  Pallas kernels  12.4 us (19%)
  waiting for transfers between devices  8.08 us (12%)
  local copies, waits for them, and re-layouts  3.42 us (5%)
    all_to_all x1, blocking collectives, on_device(): line = lax.all_to_all(line, 'freq', 0, 0, tiled=True)  15.7 us
    pallas_call x11, Pallas kernels, call(): pl.pallas_call(kernel, out_shape=out_shape, in_specs=[VMEM] * len(args) i...  12.4 us
    all_to_all x1, starting transfers between devices, on_device(): parts = lax.all_to_all(part, 'freq', 0, 0, tiled=True)  11.3 us
    all_to_all x1, blocking collectives, on_device(): stacks = lax.all_to_all(stacks, 'blk', 0, 0, tiled=True)  8.73 us
    all_to_all x1, waiting for transfers between devices, on_device(): parts = lax.all_to_all(part, 'freq', 0, 0, tiled=True)  6.29 us
    ppermute x4, starting transfers between devices, exchange(): lax.ppermute(sent[kind], 'blk', [(a, target(kind, a)) for a in range(bloc...  5.94 us
    unnamed x10, local copies, waits for them, and re-layouts  3.42 us
    ppermute x4, waiting for transfers between devices, exchange(): lax.ppermute(sent[kind], 'blk', [(a, target(kind, a)) for a in range(bloc...  1.79 us
  transfers between devices with their start and end apart: 5, of which 2 were waited for; matrix products, arithmetic and copies ran while one was open for 0% of the time, Pallas kernels for 12%

profile of v4, /device:TPU:8, one launch (start us, length us, event | category | flops | bytes accessed | tf_op | source)
XLA Modules:
  0.0 65.8 jit_solution(12610637353878750628)
XLA Ops:
  0.0 0.9 %copy-done = bf16[256,2,128]{2,1,0:T(2,128)(2,1)S(1)} copy-done((bf16[256,2,128]{2,1,0:T(2,128)(2,1)S(1)}, bf16[256,2,128]{2,1,0:T(2,128)(2,1)}, u32[]{:S(2)}) %copy-start) | copy-done | bytes 131096
  0.9 0.8 %shard_map.55 = (f32[32,1,256]{2,1,0:T(1,128)}, bf16[256,256]{1,0:T(8,128)(2,1)S(1)}) custom-call(bf16[512,128]{1,0:T(8,128)(2,1)S(1)} %bitcast.4), custom_call_target="tpu_custom_call" | custom-call | flops 1000000 | bytes 300000 | tf_op jit(solution)/shard_map/pallas_call | solution.py:51
  1.7 11.3 %all-to-all-start = ((f32[32,1,256]{2,1,0:T(1,128)}), f32[32,1,256]{2,1,0:T(1,128)S(1)}, u32[]{:S(2)}, u32[]{:S(2)}) async-start(f32[32,1,256]{2,1,0:T(1,128)} %get-tuple-element.13.part_ref), calls=%async_computation | async-start | bytes 65536 | tf_op jit(solution)/shard_map/all_to_all | solution.py:216
  13.0 0.8 %copy-done.1 = s32[1,8,2048]{2,1,0:T(8,128)S(1)} copy-done((s32[1,8,2048]{2,1,0:T(8,128)S(1)}, s32[1,8,2048]{2,1,0:T(8,128)}, u32[]{:S(2)}) %copy-start.1) | copy-done | bytes 65560
  13.9 0.8 %copy-done.2 = s32[1,8,2048]{2,1,0:T(8,128)S(1)} copy-done((s32[1,8,2048]{2,1,0:T(8,128)S(1)}, s32[1,8,2048]{2,1,0:T(8,128)}, u32[]{:S(2)}) %copy-start.2) | copy-done | bytes 65560
  14.7 0.8 %copy-done.3 = s32[1,8,2048]{2,1,0:T(8,128)S(1)} copy-done((s32[1,8,2048]{2,1,0:T(8,128)S(1)}, s32[1,8,2048]{2,1,0:T(8,128)}, u32[]{:S(2)}) %copy-start.3) | copy-done | bytes 65560
  15.6 1.3 %shard_map.56 = (bf16[256,4096]{1,0:T(8,128)(2,1)S(1)}, bf16[8,32,256]{2,1,0:T(8,128)(2,1)S(1)}) custom-call(s32[1]{0:T(128)} %bitcast.1.me_ref, s32[1,8,2048]{2,1,0:T(8,128)S(1)} %copy-done.1, s32[1,8,2048]{2,1,0:T(8,128)S(1)} %copy-done.2, s32[1,8,2048]{2,1,0:T(8,128)S(1)} %copy-done.3, f32[32,1,256]{2,1,0:T(1,128)} %get-tuple-element.13.part_ref), custom_call_target="tpu_custom_call" | custom-call | flops 10000000 | bytes 8000000 | tf_op jit(solution)/shard_map/pallas_call | solution.py:51
  16.8 6.3 %all-to-all-done.parts_ref = f32[32,1,256]{2,1,0:T(1,128)S(1)} async-done(((f32[32,1,256]{2,1,0:T(1,128)}), f32[32,1,256]{2,1,0:T(1,128)S(1)}, u32[]{:S(2)}, u32[]{:S(2)}) %all-to-all-start) | async-done | bytes 32800 | tf_op jit(solution)/shard_map/all_to_all | solution.py:216
  23.1 0.3 shard_map.57
  23.4 1.7 %collective-permute-start = (bf16[288,256]{1,0:T(8,128)(2,1)S(1)}, bf16[288,256]{1,0:T(8,128)(2,1)S(1)}, u32[]{:S(2)}, u32[]{:S(2)}) collective-permute-start(bf16[288,256]{1,0:T(8,128)(2,1)S(1)} %get-tuple-element.17), channel_id=1, source_target_pairs={{0,32},{32,64},{64,96},{96,0},{128,160},{160,192},{192,224},{224,1... | collective-permute-start | bytes 442376 | tf_op jit(solution)/shard_map/ppermute | solution.py:236
  25.1 0.6 collective-permute-start.1
  25.7 1.1 %shard_map.58.refs_0_ = f32[64,256]{1,0:T(8,128)S(1)} custom-call(bf16[256,256]{1,0:T(8,128)(2,1)S(1)} %get-tuple-element.16.refs_0_.refs_1_, bf16[8,32,256]{2,1,0:T(8,128)(2,1)S(1)} %get-tuple-element.15.rows_ref.refs_1_.refs_2_), custom_call_target="tpu_custom_call" | custom-call | flops 1200000000 | bytes 1000000 | tf_op jit(solution)/shard_map/pallas_call | solution.py:51
  26.8 1.4 %collective-permute-start.2 = (bf16[288,256]{1,0:T(8,128)(2,1)S(1)}, bf16[288,256]{1,0:T(8,128)(2,1)S(1)}, u32[]{:S(2)}, u32[]{:S(2)}) collective-permute-start(bf16[288,256]{1,0:T(8,128)(2,1)S(1)} %get-tuple-element.18), channel_id=1, source_target_pairs={{0,224},{32,128},{64,160},{96,192},{128,96},{160,0},{192,32},{224,... | collective-permute-start | bytes 442376 | tf_op jit(solution)/shard_map/ppermute | solution.py:236
  28.2 2.3 %collective-permute-start.3 = (bf16[288,256]{1,0:T(8,128)(2,1)S(1)}, bf16[288,256]{1,0:T(8,128)(2,1)S(1)}, u32[]{:S(2)}, u32[]{:S(2)}) collective-permute-start(bf16[288,256]{1,0:T(8,128)(2,1)S(1)} %get-tuple-element.19), channel_id=1, source_target_pairs={{0,64},{32,96},{64,128},{96,160},{128,192},{160,224},{192,0},{224,... | collective-permute-start | bytes 442376 | tf_op jit(solution)/shard_map/ppermute | solution.py:236
  30.5 2.2 %shard_map.59.refs_0_ = f32[64,256]{1,0:T(8,128)S(1)} custom-call(f32[64,256]{1,0:T(8,128)S(1)} %shard_map.58.refs_0_, bf16[256,256]{1,0:T(8,128)(2,1)S(1)} %get-tuple-element.16.refs_0_.refs_1_, bf16[8,32,256]{2,1,0:T(8,128)(2,1)S(1)} %get-tuple-element.15.rows_ref.refs_1_.refs_2_, bf16[288,256]{1,0:T(8,128)(2,1)S(1)} %collective-permute-done.refs_3_), custom_call_target="tpu_custom_call" | custom-call | flops 1200000000 | bytes 1000000 | tf_op jit(solution)/shard_map/pallas_call | solution.py:51
  32.7 1.1 %shard_map.60.refs_0_ = f32[64,256]{1,0:T(8,128)S(1)} custom-call(f32[64,256]{1,0:T(8,128)S(1)} %shard_map.59.refs_0_, bf16[256,256]{1,0:T(8,128)(2,1)S(1)} %get-tuple-element.16.refs_0_.refs_1_, bf16[8,32,256]{2,1,0:T(8,128)(2,1)S(1)} %get-tuple-element.15.rows_ref.refs_1_.refs_2_, bf16[256,256]{1,0:T(8,128)(2,1)S(1)} %collective-permute-done.1.refs_3_), custom_call_target="tpu_custom_call" | custom-call | flops 1200000000 | bytes 1000000 | tf_op jit(solution)/shard_map/pallas_call | solution.py:51
  33.8 1.8 %collective-permute-done.2.refs_3_ = bf16[288,256]{1,0:T(8,128)(2,1)S(1)} collective-permute-done((bf16[288,256]{1,0:T(8,128)(2,1)S(1)}, bf16[288,256]{1,0:T(8,128)(2,1)S(1)}, u32[]{:S(2)}, u32[]{:S(2)}) %collective-permute-start.2) | collective-permute-done | bytes 147488 | tf_op jit(solution)/shard_map/ppermute | solution.py:236
  35.6 2.2 %shard_map.61.after_ref.refs_0_ = f32[64,256]{1,0:T(8,128)S(1)} custom-call(f32[64,256]{1,0:T(8,128)S(1)} %shard_map.60.refs_0_, bf16[256,256]{1,0:T(8,128)(2,1)S(1)} %get-tuple-element.16.refs_0_.refs_1_, bf16[8,32,256]{2,1,0:T(8,128)(2,1)S(1)} %get-tuple-element.15.rows_ref.refs_1_.refs_2_, bf16[288,256]{1,0:T(8,128)(2,1)S(1)} %collective-permute-done.2.refs_3_), custom_call_target="tpu_custom_call" | custom-call | flops 1200000000 | bytes 1000000 | tf_op jit(solution)/shard_map/pallas_call | solution.py:51
  37.8 0.1 shard_map.62.refs_4_
  37.9 2.3 %shard_map.63 = bf16[8,16,256]{2,1,0:T(8,128)(2,1)S(1)} custom-call(f32[64,256]{1,0:T(8,128)S(1)} %shard_map.61.after_ref.refs_0_, bf16[256,256]{1,0:T(8,128)(2,1)S(1)} %get-tuple-element.16.refs_0_.refs_1_, bf16[8,32,256]{2,1,0:T(8,128)(2,1)S(1)} %get-tuple-element.15.rows_ref.refs_1_.refs_2_, bf16[288,256]{1,0:T(8,128)(2,1)S(1)} %collective-permute-done.3.refs_3_, ...), custom_call_target="tpu_custom_call" | custom-call | flops 1200000000 | bytes 1000000 | tf_op jit(solution)/shard_map/pallas_call | solution.py:51
  40.2 8.7 %all_to_all.15.got_ref = bf16[8,16,256]{2,1,0:T(8,128)(2,1)S(1)} all-to-all(bf16[8,16,256]{2,1,0:T(8,128)(2,1)S(1)} %shard_map.63), channel_id=1, replica_groups=mesh['blk'=8,'freq'=32] {'blk'}, dimensions={0} | all-to-all | bytes 131072 | tf_op jit(solution)/shard_map/all_to_all | solution.py:250
  48.9 0.4 shard_map.64
  49.4 15.7 %all_to_all.16.got_ref = bf16[32,16,128]{2,1,0:T(8,128)(2,1)S(1)} all-to-all(bf16[32,16,128]{2,1,0:T(8,128)(2,1)S(1)} %shard_map.64), channel_id=1, replica_groups=mesh['blk'=8,'freq'=32] {'freq'}, dimensions={0} | all-to-all | bytes 262144 | tf_op jit(solution)/shard_map/all_to_all | solution.py:255
  65.1 0.6 shard_map.65
  (9 shorter events, 0.0 us)
Async XLA Ops:
  0.0 0.9 %copy-start = (bf16[256,2,128]{2,1,0:T(2,128)(2,1)S(1)}, bf16[256,2,128]{2,1,0:T(2,128)(2,1)}, u32[]{:S(2)}) copy-start(bf16[256,2,128]{2,1,0:T(2,128)(2,1)} %param.5) | copy-start | bytes 393220
  1.7 21.4 %all-to-all-start = ((f32[32,1,256]{2,1,0:T(1,128)}), f32[32,1,256]{2,1,0:T(1,128)S(1)}, u32[]{:S(2)}, u32[]{:S(2)}) async-start(f32[32,1,256]{2,1,0:T(1,128)} %get-tuple-element.13.part_ref), calls=%async_computation | async-start | bytes 65536 | tf_op jit(solution)/shard_map/all_to_all | solution.py:216
  13.0 0.8 %copy-start.1 = (s32[1,8,2048]{2,1,0:T(8,128)S(1)}, s32[1,8,2048]{2,1,0:T(8,128)}, u32[]{:S(2)}) copy-start(s32[1,8,2048]{2,1,0:T(8,128)} %first_ref.1) | copy-start | bytes 196612
  13.9 0.8 %copy-start.2 = (s32[1,8,2048]{2,1,0:T(8,128)S(1)}, s32[1,8,2048]{2,1,0:T(8,128)}, u32[]{:S(2)}) copy-start(s32[1,8,2048]{2,1,0:T(8,128)} %second_ref.1) | copy-start | bytes 196612
  14.7 0.8 %copy-start.3 = (s32[1,8,2048]{2,1,0:T(8,128)S(1)}, s32[1,8,2048]{2,1,0:T(8,128)}, u32[]{:S(2)}) copy-start(s32[1,8,2048]{2,1,0:T(8,128)} %bin_ref.1) | copy-start | bytes 196612
  23.4 7.0 %collective-permute-start = (bf16[288,256]{1,0:T(8,128)(2,1)S(1)}, bf16[288,256]{1,0:T(8,128)(2,1)S(1)}, u32[]{:S(2)}, u32[]{:S(2)}) collective-permute-start(bf16[288,256]{1,0:T(8,128)(2,1)S(1)} %get-tuple-element.17), channel_id=1, source_target_pairs={{0,32},{32,64},{64,96},{96,0},{128,160},{160,192},{192,224},{224,1... | collective-permute-start | bytes 442376 | tf_op jit(solution)/shard_map/ppermute | solution.py:236
  25.1 7.6 %collective-permute-start.1 = (bf16[256,256]{1,0:T(8,128)(2,1)S(1)}, bf16[256,256]{1,0:T(8,128)(2,1)S(1)}, u32[]{:S(2)}, u32[]{:S(2)}) collective-permute-start(bf16[256,256]{1,0:T(8,128)(2,1)S(1)} %get-tuple-element.16.refs_0_.refs_1_), channel_id=1, source_target_pairs={{0,128},{32,160},{64,192},{96,224},{128,0},{160,32},{192,64},{224,... | collective-permute-start | bytes 393224 | tf_op jit(solution)/shard_map/ppermute | solution.py:236
  26.8 8.8 %collective-permute-start.2 = (bf16[288,256]{1,0:T(8,128)(2,1)S(1)}, bf16[288,256]{1,0:T(8,128)(2,1)S(1)}, u32[]{:S(2)}, u32[]{:S(2)}) collective-permute-start(bf16[288,256]{1,0:T(8,128)(2,1)S(1)} %get-tuple-element.18), channel_id=1, source_target_pairs={{0,224},{32,128},{64,160},{96,192},{128,96},{160,0},{192,32},{224,... | collective-permute-start | bytes 442376 | tf_op jit(solution)/shard_map/ppermute | solution.py:236
  28.2 9.7 %collective-permute-start.3 = (bf16[288,256]{1,0:T(8,128)(2,1)S(1)}, bf16[288,256]{1,0:T(8,128)(2,1)S(1)}, u32[]{:S(2)}, u32[]{:S(2)}) collective-permute-start(bf16[288,256]{1,0:T(8,128)(2,1)S(1)} %get-tuple-element.19), channel_id=1, source_target_pairs={{0,64},{32,96},{64,128},{96,160},{128,192},{160,224},{192,0},{224,... | collective-permute-start | bytes 442376 | tf_op jit(solution)/shard_map/ppermute | solution.py:236
  33.8 4.0 %copy-start.4 = (s32[64]{0:T(128)S(1)}, s32[64]{0:T(128)}, u32[]{:S(2)}) copy-start(s32[64]{0:T(128)} %param.9) | copy-start | bytes 772

commit v5 on v4

--- a/solution.py
+++ b/solution.py
@@ -20,27 +20,18 @@
 SMEM = pl.BlockSpec(memory_space=pltpu.SMEM)
 
 
-def target(kind, a):
-    if kind == "beside":
-        return a - a % 4 + (a + 1) % 4
-    if kind == "corner":
-        return (a - a % 4 + 4) % 8 + (a + 3) % 4
-    if kind == "across":
-        return (a + 4) % 8
-    return (a + 2) % 8
-
-
-def source(kind, a):
-    if kind == "beside":
-        return a - a % 4 + (a + 3) % 4
-    if kind == "corner":
-        return (a - a % 4 + 4) % 8 + (a + 1) % 4
-    if kind == "across":
-        return (a + 4) % 8
-    return (a + 6) % 8
-
-
-TWO_WAY = ("beside", "corner", "far")
+STEPS = {"beside": (0, 3), "across": (1, 0), "two": (0, 2)}
+CARRIED = {"beside": ("own", "across"), "across": ("beside", "two"), "two": ()}
+
+
+def place(kind, a):
+    dx, dy = STEPS.get(kind, (0, 0))
+    return (a - a % 4 + 4 * dx) % 8 + (a + dy) % 4
+
+
+def reader(kind, a):
+    dx, dy = STEPS[kind]
+    return (a - a % 4 + 4 * dx) % 8 + (a + 4 - dy) % 4
 
 
 def shape(dims, dtype):
@@ -123,9 +114,12 @@
     white = (x_ref[...].astype(F32) / rms).astype(BF16)
     own_ref[...] = white
     me = lax.axis_index("blk")
-    for kind, ref in zip(TWO_WAY, sent):
+    for kind, ref in zip(STEPS, sent):
         ref[:256, :] = white
-        ref[256:, :] = rows_ref[lax.rem(me - target(kind, me) + 8, 8)]
+        for k, other in enumerate(CARRIED[kind]):
+            partner = place(other, reader(kind, me))
+            first = 256 + 3 * CHUNKS * k
+            ref[first : first + 3 * CHUNKS, :] = rows_ref[(me - partner + 8) % 8, : 3 * CHUNKS]
 
 
 def column_onehot(col):
@@ -152,34 +146,35 @@
     return jnp.dot(jnp.concatenate(onehot, 1), cross, preferred_element_type=F32)
 
 
-def pair_kernel(kinds, first, last, *refs):
+def pair_kernel(jobs, kinds, first, last, *refs):
     refs = list(refs)
     acc = None if first else refs.pop(0)[...]
-    own_ref, rows_ref = refs[:2]
-    got = refs[2 : 2 + len(kinds)]
+    rows_ref = refs.pop(0)
+    held = dict(zip(kinds, refs))
     out_ref = refs[-1]
-    if first:
-        acc = add_list(rows_ref[0].astype(F32), own_ref[...], own_ref[...])
     me = lax.axis_index("blk")
-    for kind, got_ref in zip(kinds, got):
-        mine = rows_ref[lax.rem(me - source(kind, me) + 8, 8)].astype(F32)
-        acc = acc + add_list(mine, own_ref[...], got_ref[:256, :])
-        if kind in TWO_WAY:
-            acc = acc + add_list(got_ref[256:, :].astype(F32), got_ref[:256, :], own_ref[...])
+    for one, other in jobs:
+        if one == "own":
+            rows = rows_ref[(me - place(other, me) + 8) % 8].astype(F32)
+        else:
+            start = 256 + 3 * CHUNKS * CARRIED[one].index(other)
+            rows = held[one][start : start + 3 * CHUNKS, :].astype(F32)
+        part = add_list(rows, held[one][:256, :], held[other][:256, :])
+        acc = part if acc is None else acc + part
     if last:
-        pick = refs[2 + len(kinds)][...]
-        owned = jnp.dot(pick, acc.astype(BF16), preferred_element_type=F32)
+        owned = jnp.dot(refs[-2][...], acc.astype(BF16), preferred_element_type=F32)
         acc = owned.reshape(out_ref.shape)
     out_ref[...] = acc.astype(out_ref.dtype)
 
 
-def pair_call(kinds, out_shape, acc, own, lists, got, select):
+def pair_call(jobs, out_shape, acc, rows, held, select):
     first, last = acc is None, select is not None
+    kinds = tuple(dict.fromkeys(kind for job in jobs for kind in job))
     args = [] if first else [acc]
-    args += [own, lists, *got]
+    args += [rows, *(held[kind] for kind in kinds)]
     args += [select] if last else []
-    kernel = functools.partial(pair_kernel, kinds, first, last)
-    return call(kernel, out_shape, args, 20, 1_200_000_000 * max(len(kinds), 1), 1_000_000)
+    kernel = functools.partial(pair_kernel, jobs, kinds, first, last)
+    return call(kernel, out_shape, args, 20, 600_000_000 * len(jobs), 1_000_000)
 
 
 def lag_kernel(got_ref, factors_ref, out_ref):
@@ -226,27 +221,31 @@
 
     own, *sent = call(
         white_kernel,
-        [shape((sensors, width), BF16)] + [shape((sensors + 32, width), BF16)] * 3,
+        [shape((sensors, width), BF16)]
+        + [shape((sensors + 3 * CHUNKS * len(CARRIED[kind]), width), BF16) for kind in STEPS],
         (parts, flat, rows), 4, 1_000_000, 800_000,
     )
 
-    sent = dict(zip(TWO_WAY, sent), across=own)
-
-    def exchange(kind):
-        return lax.ppermute(sent[kind], "blk", [(a, target(kind, a)) for a in range(blocks)])
-
-    got = {kind: exchange(kind) for kind in ("far", "beside", "corner", "across")}
+    sent = dict(zip(STEPS, sent))
+    held = {"own": own}
+    for kind in STEPS:
+        hops = [(a, reader(kind, a)) for a in range(blocks)]
+        held[kind] = lax.ppermute(sent[kind], "blk", hops)
 
     acc_shape = shape((NB, width), F32)
-    acc = pair_call((), acc_shape, None, own, rows, (), None)
-    for kind in ("beside", "across", "corner"):
-        acc = pair_call((kind,), acc_shape, acc, own, rows, (got[kind],), None)
+    acc = pair_call((("own", "own"),), acc_shape, None, rows, held, None)
+    for jobs in (
+        (("own", "beside"), ("beside", "own")),
+        (("own", "across"), ("across", "beside"), ("beside", "across")),
+    ):
+        acc = pair_call(jobs, acc_shape, acc, rows, held, None)
     select = call(
         select_kernel, shape((2 * NB, NB), BF16), (bin_owner.reshape(1, NB), acc), 2, 100_000, 30_000,
         specs=[VMEM, anywhere],
     )
+    jobs = (("own", "two"), ("across", "two"))
     stacks_shape = shape((blocks, slots_each, width), BF16)
-    stacks = pair_call(("far",), stacks_shape, acc, own, rows, (got["far"],), select)
+    stacks = pair_call(jobs, stacks_shape, acc, rows, held, select)
     stacks = lax.all_to_all(stacks, "blk", 0, 0, tiled=True)
 
     line = call(

time: 66.9 us -> 68 us (1.016)
  blocking collectives: 24.5 us -> 28.1 us
  starting transfers between devices: 17.3 us -> 14.5 us
    all_to_all x1, blocking collectives: 8.73 us -> 11.7 us  [on_device(): stacks = lax.all_to_all(stacks, 'blk', 0, 0, tiled=True)]
    ppermute x4 -> x3, starting transfers between devices: 5.94 us -> 3.19 us  [on_device(): held[kind] = lax.ppermute(sent[kind], 'blk', hops)]
    ppermute x4 -> x3, waiting for transfers between devices: 1.79 us -> 2.01 us  [on_device(): held[kind] = lax.ppermute(sent[kind], 'blk', hops)]
    pallas_call x11 -> x10, Pallas kernels: 12.4 us -> 12.4 us  [call(): pl.pallas_call(kernel, out_shape=out_shape, in_specs=[VMEM] * len(args) i...]
  transfers between devices with their start and end apart: 5 -> 4, of which waited for: 2 -> 2; matrix products, arithmetic and copies ran while one was open for 0% -> 0% of each run, Pallas kernels for 12% -> 12%
where the time goes in v5:
time: 68 us; the launch traced here: 66.8 us
  blocking collectives  28.1 us (41%)
  starting transfers between devices  14.5 us (21%)
  Pallas kernels  12.4 us (18%)
  waiting for transfers between devices  8.31 us (12%)
  local copies, waits for them, and re-layouts  3.42 us (5%)
    all_to_all x1, blocking collectives, on_device(): line = lax.all_to_all(line, 'freq', 0, 0, tiled=True)  16.4 us
    pallas_call x10, Pallas kernels, call(): pl.pallas_call(kernel, out_shape=out_shape, in_specs=[VMEM] * len(args) i...  12.4 us
    all_to_all x1, blocking collectives, on_device(): stacks = lax.all_to_all(stacks, 'blk', 0, 0, tiled=True)  11.7 us
    all_to_all x1, starting transfers between devices, on_device(): parts = lax.all_to_all(part, 'freq', 0, 0, tiled=True)  11.3 us
    all_to_all x1, waiting for transfers between devices, on_device(): parts = lax.all_to_all(part, 'freq', 0, 0, tiled=True)  6.3 us
    unnamed x10, local copies, waits for them, and re-layouts  3.42 us
    ppermute x3, starting transfers between devices, on_device(): held[kind] = lax.ppermute(sent[kind], 'blk', hops)  3.19 us
    ppermute x3, waiting for transfers between devices, on_device(): held[kind] = lax.ppermute(sent[kind], 'blk', hops)  2.01 us
  transfers between devices with their start and end apart: 4, of which 2 were waited for; matrix products, arithmetic and copies ran while one was open for 0% of the time, Pallas kernels for 12%

profile of v5, /device:TPU:8, one launch (start us, length us, event | category | flops | bytes accessed | tf_op | source)
XLA Modules:
  0.0 66.8 jit_solution(8982311361165504578)
XLA Ops:
  0.0 0.9 %copy-done = bf16[256,2,128]{2,1,0:T(2,128)(2,1)S(1)} copy-done((bf16[256,2,128]{2,1,0:T(2,128)(2,1)S(1)}, bf16[256,2,128]{2,1,0:T(2,128)(2,1)}, u32[]{:S(2)}) %copy-start) | copy-done | bytes 131096
  0.9 0.8 %shard_map.55 = (f32[32,1,256]{2,1,0:T(1,128)}, bf16[256,256]{1,0:T(8,128)(2,1)S(1)}) custom-call(bf16[512,128]{1,0:T(8,128)(2,1)S(1)} %bitcast.4), custom_call_target="tpu_custom_call" | custom-call | flops 1000000 | bytes 300000 | tf_op jit(solution)/shard_map/pallas_call | solution.py:42
  1.7 11.3 %all-to-all-start = ((f32[32,1,256]{2,1,0:T(1,128)}), f32[32,1,256]{2,1,0:T(1,128)S(1)}, u32[]{:S(2)}, u32[]{:S(2)}) async-start(f32[32,1,256]{2,1,0:T(1,128)} %get-tuple-element.13.part_ref), calls=%async_computation | async-start | bytes 65536 | tf_op jit(solution)/shard_map/all_to_all | solution.py:211
  13.0 0.0 copy-start.1
  13.0 0.8 %copy-done.1 = s32[1,8,2048]{2,1,0:T(8,128)S(1)} copy-done((s32[1,8,2048]{2,1,0:T(8,128)S(1)}, s32[1,8,2048]{2,1,0:T(8,128)}, u32[]{:S(2)}) %copy-start.1) | copy-done | bytes 65560
  13.9 0.8 %copy-done.2 = s32[1,8,2048]{2,1,0:T(8,128)S(1)} copy-done((s32[1,8,2048]{2,1,0:T(8,128)S(1)}, s32[1,8,2048]{2,1,0:T(8,128)}, u32[]{:S(2)}) %copy-start.2) | copy-done | bytes 65560
  14.7 0.8 %copy-done.3 = s32[1,8,2048]{2,1,0:T(8,128)S(1)} copy-done((s32[1,8,2048]{2,1,0:T(8,128)S(1)}, s32[1,8,2048]{2,1,0:T(8,128)}, u32[]{:S(2)}) %copy-start.3) | copy-done | bytes 65560
  15.6 1.3 %shard_map.56 = (bf16[256,4096]{1,0:T(8,128)(2,1)S(1)}, bf16[8,32,256]{2,1,0:T(8,128)(2,1)S(1)}) custom-call(s32[1]{0:T(128)} %bitcast.me_ref, s32[1,8,2048]{2,1,0:T(8,128)S(1)} %copy-done.1, s32[1,8,2048]{2,1,0:T(8,128)S(1)} %copy-done.2, s32[1,8,2048]{2,1,0:T(8,128)S(1)} %copy-done.3, f32[32,1,256]{2,1,0:T(1,128)} %get-tuple-element.13.part_ref), custom_call_target="tpu_custom_call" | custom-call | flops 10000000 | bytes 8000000 | tf_op jit(solution)/shard_map/pallas_call | solution.py:42
  16.8 6.3 %all-to-all-done.parts_ref = f32[32,1,256]{2,1,0:T(1,128)S(1)} async-done(((f32[32,1,256]{2,1,0:T(1,128)}), f32[32,1,256]{2,1,0:T(1,128)S(1)}, u32[]{:S(2)}, u32[]{:S(2)}) %all-to-all-start) | async-done | bytes 32800 | tf_op jit(solution)/shard_map/all_to_all | solution.py:211
  23.1 0.3 shard_map.57
  23.4 1.7 %collective-permute-start = (bf16[304,256]{1,0:T(8,128)(2,1)S(1)}, bf16[304,256]{1,0:T(8,128)(2,1)S(1)}, u32[]{:S(2)}, u32[]{:S(2)}) collective-permute-start(bf16[304,256]{1,0:T(8,128)(2,1)S(1)} %get-tuple-element.17), channel_id=1, source_target_pairs={{0,32},{32,64},{64,96},{96,0},{128,160},{160,192},{192,224},{224,1... | collective-permute-start | bytes 466952 | tf_op jit(solution)/shard_map/ppermute | solution.py:233
  25.1 0.9 %collective-permute-start.2 = (bf16[256,256]{1,0:T(8,128)(2,1)S(1)}, bf16[256,256]{1,0:T(8,128)(2,1)S(1)}, u32[]{:S(2)}, u32[]{:S(2)}) collective-permute-start(bf16[256,256]{1,0:T(8,128)(2,1)S(1)} %get-tuple-element.19), channel_id=1, source_target_pairs={{0,64},{32,96},{64,0},{96,32},{128,192},{160,224},{192,128},{224,1... | collective-permute-start | bytes 393224 | tf_op jit(solution)/shard_map/ppermute | solution.py:233
  26.0 0.6 collective-permute-start.1
  26.6 1.1 %shard_map.58.refs_0_ = f32[64,256]{1,0:T(8,128)S(1)} custom-call(bf16[8,32,256]{2,1,0:T(8,128)(2,1)S(1)} %get-tuple-element.14.rows_ref.refs_0_.refs_1_, bf16[256,256]{1,0:T(8,128)(2,1)S(1)} %get-tuple-element.16.refs_1_.refs_2_), custom_call_target="tpu_custom_call" | custom-call | flops 600000000 | bytes 1000000 | tf_op jit(solution)/shard_map/pallas_call | solution.py:42
  27.8 2.0 %collective-permute-done.refs_3_.refs_4_ = bf16[304,256]{1,0:T(8,128)(2,1)S(1)} collective-permute-done((bf16[304,256]{1,0:T(8,128)(2,1)S(1)}, bf16[304,256]{1,0:T(8,128)(2,1)S(1)}, u32[]{:S(2)}, u32[]{:S(2)}) %collective-permute-start) | collective-permute-done | bytes 155680 | tf_op jit(solution)/shard_map/ppermute | solution.py:233
  29.8 2.2 %shard_map.59.refs_0_ = f32[64,256]{1,0:T(8,128)S(1)} custom-call(f32[64,256]{1,0:T(8,128)S(1)} %shard_map.58.refs_0_, bf16[8,32,256]{2,1,0:T(8,128)(2,1)S(1)} %get-tuple-element.14.rows_ref.refs_0_.refs_1_, bf16[256,256]{1,0:T(8,128)(2,1)S(1)} %get-tuple-element.16.refs_1_.refs_2_, bf16[304,256]{1,0:T(8,128)(2,1)S(1)} %collective-permute-done.refs_3_.refs_4_), custom_call_target="tpu_custom_call" | custom-call | flops 1200000000 | bytes 1000000 | tf_op jit(solution)/shard_map/pallas_call | solution.py:42
  31.9 0.0 copy-start.4
  32.0 3.2 %shard_map.60.after_ref.refs_0_ = f32[64,256]{1,0:T(8,128)S(1)} custom-call(f32[64,256]{1,0:T(8,128)S(1)} %shard_map.59.refs_0_, bf16[8,32,256]{2,1,0:T(8,128)(2,1)S(1)} %get-tuple-element.14.rows_ref.refs_0_.refs_1_, bf16[256,256]{1,0:T(8,128)(2,1)S(1)} %get-tuple-element.16.refs_1_.refs_2_, bf16[304,256]{1,0:T(8,128)(2,1)S(1)} %collective-permute-done.1.refs_3_.refs_4_, ...), custom_call_target="tpu_custom_call" | custom-call | flops 1800000000 | bytes 1000000 | tf_op jit(solution)/shard_map/pallas_call | solution.py:42
  35.2 0.1 shard_map.61.refs_5_
  35.3 2.3 %shard_map.62 = bf16[8,16,256]{2,1,0:T(8,128)(2,1)S(1)} custom-call(f32[64,256]{1,0:T(8,128)S(1)} %shard_map.60.after_ref.refs_0_, bf16[8,32,256]{2,1,0:T(8,128)(2,1)S(1)} %get-tuple-element.14.rows_ref.refs_0_.refs_1_, bf16[256,256]{1,0:T(8,128)(2,1)S(1)} %get-tuple-element.16.refs_1_.refs_2_, bf16[256,256]{1,0:T(8,128)(2,1)S(1)} %collective-permute-done.2.refs_3_, ...), custom_call_target="tpu_custom_call" | custom-call | flops 1200000000 | bytes 1000000 | tf_op jit(solution)/shard_map/pallas_call | solution.py:42
  37.6 11.7 %all_to_all.15.got_ref = bf16[8,16,256]{2,1,0:T(8,128)(2,1)S(1)} all-to-all(bf16[8,16,256]{2,1,0:T(8,128)(2,1)S(1)} %shard_map.62), channel_id=1, replica_groups=mesh['blk'=8,'freq'=32] {'blk'}, dimensions={0} | all-to-all | bytes 131072 | tf_op jit(solution)/shard_map/all_to_all | solution.py:249
  49.4 0.4 shard_map.63
  49.8 16.4 %all_to_all.16.got_ref = bf16[32,16,128]{2,1,0:T(8,128)(2,1)S(1)} all-to-all(bf16[32,16,128]{2,1,0:T(8,128)(2,1)S(1)} %shard_map.63), channel_id=1, replica_groups=mesh['blk'=8,'freq'=32] {'freq'}, dimensions={0} | all-to-all | bytes 262144 | tf_op jit(solution)/shard_map/all_to_all | solution.py:254
  66.2 0.6 shard_map.64
  (6 shorter events, 0.0 us)
Async XLA Ops:
  0.0 0.9 %copy-start = (bf16[256,2,128]{2,1,0:T(2,128)(2,1)S(1)}, bf16[256,2,128]{2,1,0:T(2,128)(2,1)}, u32[]{:S(2)}) copy-start(bf16[256,2,128]{2,1,0:T(2,128)(2,1)} %param.5) | copy-start | bytes 393220
  1.7 21.4 %all-to-all-start = ((f32[32,1,256]{2,1,0:T(1,128)}), f32[32,1,256]{2,1,0:T(1,128)S(1)}, u32[]{:S(2)}, u32[]{:S(2)}) async-start(f32[32,1,256]{2,1,0:T(1,128)} %get-tuple-element.13.part_ref), calls=%async_computation | async-start | bytes 65536 | tf_op jit(solution)/shard_map/all_to_all | solution.py:211
  13.0 0.8 %copy-start.1 = (s32[1,8,2048]{2,1,0:T(8,128)S(1)}, s32[1,8,2048]{2,1,0:T(8,128)}, u32[]{:S(2)}) copy-start(s32[1,8,2048]{2,1,0:T(8,128)} %first_ref.1) | copy-start | bytes 196612
  13.9 0.8 %copy-start.2 = (s32[1,8,2048]{2,1,0:T(8,128)S(1)}, s32[1,8,2048]{2,1,0:T(8,128)}, u32[]{:S(2)}) copy-start(s32[1,8,2048]{2,1,0:T(8,128)} %second_ref.1) | copy-start | bytes 196612
  14.7 0.8 %copy-start.3 = (s32[1,8,2048]{2,1,0:T(8,128)S(1)}, s32[1,8,2048]{2,1,0:T(8,128)}, u32[]{:S(2)}) copy-start(s32[1,8,2048]{2,1,0:T(8,128)} %bin_ref.1) | copy-start | bytes 196612
  23.4 6.3 %collective-permute-start = (bf16[304,256]{1,0:T(8,128)(2,1)S(1)}, bf16[304,256]{1,0:T(8,128)(2,1)S(1)}, u32[]{:S(2)}, u32[]{:S(2)}) collective-permute-start(bf16[304,256]{1,0:T(8,128)(2,1)S(1)} %get-tuple-element.17), channel_id=1, source_target_pairs={{0,32},{32,64},{64,96},{96,0},{128,160},{160,192},{192,224},{224,1... | collective-permute-start | bytes 466952 | tf_op jit(solution)/shard_map/ppermute | solution.py:233
  25.1 10.2 %collective-permute-start.2 = (bf16[256,256]{1,0:T(8,128)(2,1)S(1)}, bf16[256,256]{1,0:T(8,128)(2,1)S(1)}, u32[]{:S(2)}, u32[]{:S(2)}) collective-permute-start(bf16[256,256]{1,0:T(8,128)(2,1)S(1)} %get-tuple-element.19), channel_id=1, source_target_pairs={{0,64},{32,96},{64,0},{96,32},{128,192},{160,224},{192,128},{224,1... | collective-permute-start | bytes 393224 | tf_op jit(solution)/shard_map/ppermute | solution.py:233
  26.0 5.9 %collective-permute-start.1 = (bf16[304,256]{1,0:T(8,128)(2,1)S(1)}, bf16[304,256]{1,0:T(8,128)(2,1)S(1)}, u32[]{:S(2)}, u32[]{:S(2)}) collective-permute-start(bf16[304,256]{1,0:T(8,128)(2,1)S(1)} %get-tuple-element.18), channel_id=1, source_target_pairs={{0,128},{32,160},{64,192},{96,224},{128,0},{160,32},{192,64},{224,... | collective-permute-start | bytes 466952 | tf_op jit(solution)/shard_map/ppermute | solution.py:233
  31.9 3.2 %copy-start.4 = (s32[64]{0:T(128)S(1)}, s32[64]{0:T(128)}, u32[]{:S(2)}) copy-start(s32[64]{0:T(128)} %param.9) | copy-start | bytes 772
